TPU v7x, 256 devices: a whole 4x4x8 slice. The times are simulated.
256 devices in a mesh: branch: 2 (over y_lo), row: 32 (over z, y_hi, core), seq: 4 (over x).
Axes of the slice: x: 4, y: 4 (y_hi: 2, y_lo: 2; y = y_hi * 2 + y_lo), z: 8, core: 2. Of those that a mesh axis runs over, the one named last changes fastest.
Arguments:
- alignment_input: bfloat16 [256, 256, 256], P('seq', 'row'), may hold values from -6 to 6
- pairwise_input: bfloat16 [128, 256, 256], P('seq', 'row'), may hold values from -30 to 30
- alignment_gain: float32 [256], replicated, may hold values from 0.25 to 1.75
- product_gain: float32 [256], replicated, may hold values from 0.25 to 1.75
- attention_weight: bfloat16 [256, 4, 256], replicated, may hold values from -0.375 to 0.375
- mixing_weight: bfloat16 [256, 256], replicated, may hold values from -0.375 to 0.375
- outer_input_weight: bfloat16 [256, 2, 32], replicated, may hold values from -0.375 to 0.375
- outer_output_weight: bfloat16 [32, 32, 128], replicated, may hold values from -3 to 3
- bias_matrix: bfloat16 [128, 8], replicated, may hold values from -6 to 6
- pairwise_gain: float32 [128], replicated, may hold values from 0.25 to 1.75
- triangle_input_weight: bfloat16 [4, 128, 128], P(None, 'seq'), may hold values from -0.5 to 0.5
- triangle_gate_weight: bfloat16 [128, 128], P('seq'), may hold values from -0.5 to 0.5
- triangle_gain: float32 [128], P('seq'), may hold values from 0.25 to 1.75
- triangle_output_weight: bfloat16 [128, 128], P(None, 'seq'), may hold values from -0.5 to 0.5
- transition_gain: float32 [128], replicated, may hold values from 0.25 to 1.75
- transition_up_weight: bfloat16 [512, 128], P('seq'), may hold values from -0.5 to 0.5
- transition_down_weight: bfloat16 [128, 512], P(None, 'seq'), may hold values from -0.25 to 0.25
Outputs:
- alignment_output: bfloat16 [256, 256, 256], P('seq', 'row', 'branch')
- pairwise_output: bfloat16 [128, 256, 256], P('seq', 'row', 'branch')
All inputs are finite; a program needn't handle non-finite values.
Results may differ from a plain program's by a relative error of at most 0.011.
Values may be sent and summed in bfloat16 or wider, within the bound.
A program may use at most 128 MiB of HBM per device.

v0:
```python
import jax
import jax.numpy as jnp
from jax import lax
from jax.sharding import PartitionSpec as P

EPSILON = 1e-05


def shifted(value, axis, by):
    length = lax.axis_size(axis)
    pairs = [(i, i + by) for i in range(length) if 0 <= i + by < length]
    return lax.ppermute(value, axis, pairs)


def from_partner(value, axis, distance):
    return lax.ppermute(value, axis, [(i, i ^ 1 << distance) for i in range(lax.axis_size(axis))])


def layer_normalize(values, axis):
    average = jnp.mean(values, axis=axis, keepdims=True)
    centred = values - average
    spread = jnp.mean(centred * centred, axis=axis, keepdims=True)
    return centred * lax.rsqrt(spread + EPSILON)


def full_channels(values):
    return lax.all_gather(values, "seq", axis=0, tiled=True)


def channel_sum(term, kept_rows):
    return lax.psum_scatter(
        term(jnp.int32(0), kept_rows * lax.axis_size("seq")), "seq", scatter_dimension=0, tiled=True
    )


def shards(
    alignment_input,
    pairwise_input,
    alignment_gain,
    product_gain,
    attention_weight,
    mixing_weight,
    outer_input_weight,
    outer_output_weight,
    bias_matrix,
    pairwise_gain,
    triangle_input_weight,
    triangle_gate_weight,
    triangle_gain,
    triangle_output_weight,
    transition_gain,
    transition_up_weight,
    transition_down_weight,
):
    local_sequences, local_rows, alignment_channels = alignment_input.shape
    chan_local = pairwise_input.shape[0]
    residues = pairwise_input.shape[2]
    pair_width, head_total = bias_matrix.shape
    latent_heads = mixing_weight.shape[0]
    head_size = latent_heads // head_total
    outer_width = outer_input_weight.shape[2]
    tri_local = triangle_input_weight.shape[1]
    trans_local = transition_up_weight.shape[0]
    seq_total = local_sequences * lax.axis_size("seq")
    path_index = lax.axis_index("branch")
    alignment_branch = path_index == 0
    query_shape = (local_sequences, local_rows, latent_heads)
    pair_shape = (chan_local, local_rows, residues)
    full_pair_shape = (pair_width, local_rows, residues)
    key_shape = (local_sequences, 2 * latent_heads, local_rows)
    gathered = full_channels(pairwise_input)

    def alignment_early():
        alignment_module = layer_normalize(alignment_input.astype(jnp.float32), 2)
        normalized_values = (alignment_module * alignment_gain).astype(jnp.bfloat16)
        outer_normalized = (alignment_module * product_gain).astype(jnp.bfloat16)
        flattened_rows = normalized_values.reshape(-1, alignment_channels)
        outer_flattened = outer_normalized.reshape(-1, alignment_channels)
        query = (
            (
                jnp.dot(flattened_rows, attention_weight[:, 0], preferred_element_type=jnp.float32)
                * head_size ** (-0.5)
            )
            .astype(jnp.bfloat16)
            .reshape(query_shape)
        )
        gate = (
            jax.nn.sigmoid(
                jnp.dot(flattened_rows, attention_weight[:, 3], preferred_element_type=jnp.float32)
            )
            .astype(jnp.bfloat16)
            .reshape(query_shape)
        )
        key_values = (
            jnp.einsum(
                "sim,mkc->skci",
                normalized_values,
                attention_weight[:, 1:3],
                preferred_element_type=jnp.float32,
            )
            .astype(jnp.bfloat16)
            .reshape(key_shape)
        )
        left = (
            jnp.dot(outer_flattened, outer_input_weight[:, 0], preferred_element_type=jnp.float32)
            .astype(jnp.bfloat16)
            .reshape(local_sequences, local_rows, outer_width)
        )
        right_cols = jnp.einsum(
            "sim,mc->sci",
            outer_normalized,
            outer_input_weight[:, 1],
            preferred_element_type=jnp.float32,
        ).astype(jnp.bfloat16)
        empty_bias = jnp.zeros((head_total, local_rows, residues), jnp.bfloat16)
        empty_pair = jnp.zeros(full_pair_shape, jnp.bfloat16)
        return (empty_bias, empty_pair, query, key_values, gate, left, right_cols)

    def pair_early():
        unit = layer_normalize(gathered.astype(jnp.float32), 0)
        plain = unit.astype(jnp.bfloat16).reshape(pair_width, -1)
        bias_rows = (
            jnp.einsum("ch,cn->hn", bias_matrix, plain, preferred_element_type=jnp.float32)
            .astype(jnp.bfloat16)
            .reshape(head_total, local_rows, residues)
        )
        tri_input = (unit * pairwise_gain[:, None, None]).astype(jnp.bfloat16)
        empty_query = jnp.zeros(query_shape, jnp.bfloat16)
        empty_keys = jnp.zeros(key_shape, jnp.bfloat16)
        empty_left = jnp.zeros((local_sequences, local_rows, outer_width), jnp.bfloat16)
        empty_right = jnp.zeros((local_sequences, outer_width, local_rows), jnp.bfloat16)
        return (bias_rows, tri_input, empty_query, empty_keys, empty_query, empty_left, empty_right)

    bias_local, tri_input, query, key_values, gate, left, right_cols = lax.cond(
        alignment_branch, alignment_early, pair_early
    )
    bias_recv = shifted(bias_local, "branch", -1)
    query_heads = query.reshape(local_sequences, local_rows, head_total, head_size).transpose(
        0, 2, 1, 3
    )

    def fold_real(running, shard_part):
        highest, totals, weighted = running
        columns = shard_part.shape[2]
        keys_part = shard_part[:, :latent_heads].reshape(
            local_sequences, head_total, head_size, columns
        )
        values_part = shard_part[:, latent_heads:].reshape(
            local_sequences, head_total, head_size, columns
        )
        bias_part = bias_recv.astype(jnp.float32)
        scores = (
            jnp.einsum(
                "shid,shdj->shij", query_heads, keys_part, preferred_element_type=jnp.float32
            )
            + bias_part[None]
        )
        raised = jnp.maximum(highest, jnp.max(scores, axis=3))
        weights = jnp.exp(scores - raised[..., None])
        totals = jnp.sum(weights, axis=3)
        weighted = jnp.einsum(
            "shij,shdj->shid",
            weights.astype(jnp.bfloat16),
            values_part,
            preferred_element_type=jnp.float32,
        )
        return (raised, totals, weighted)

    initial = (
        jnp.full((local_sequences, head_total, local_rows), -1e30, jnp.float32),
        jnp.zeros((local_sequences, head_total, local_rows), jnp.float32),
        jnp.zeros((local_sequences, head_total, local_rows, head_size), jnp.float32),
    )
    shard_part = lax.all_gather(key_values, "row", axis=2, tiled=True)
    highest, totals, weighted = lax.cond(
        alignment_branch, lambda: fold_real(initial, shard_part), lambda: initial
    )
    safe_totals = jnp.where(totals > 0, totals, 1.0)
    attended = (weighted / safe_totals[..., None]).transpose(0, 2, 1, 3).reshape(query_shape)
    mixed_heads = (gate.astype(jnp.float32) * attended).astype(jnp.bfloat16)
    right_full = lax.all_gather(right_cols, "row", axis=2, tiled=True)
    right_matrix = right_full.reshape(local_sequences * outer_width, residues)
    spread = lax.cond(
        alignment_branch,
        lambda: jnp.einsum(
            "sic,cdo->oisd", left, outer_output_weight, preferred_element_type=jnp.float32
        ).astype(jnp.bfloat16),
        lambda: jnp.zeros((pair_width, local_rows, local_sequences, outer_width), jnp.bfloat16),
    )

    def outer_term(amount):
        spread_part = spread.reshape(amount * local_rows, local_sequences * outer_width)
        return jnp.dot(spread_part, right_matrix, preferred_element_type=jnp.float32).reshape(
            amount, local_rows, residues
        )

    tri_flat = tri_input.reshape(pair_width, -1)

    def pair_operands():
        linear = jnp.dot(
            triangle_input_weight.reshape(4 * tri_local, pair_width),
            tri_flat,
            preferred_element_type=jnp.float32,
        )
        linear = linear.reshape(4, tri_local, local_rows, residues)
        left_part = (linear[0] * jax.nn.sigmoid(linear[1])).astype(jnp.bfloat16)
        right_part = (linear[2] * jax.nn.sigmoid(linear[3])).astype(jnp.bfloat16)
        return (left_part, right_part)

    def empty_operands():
        empty = jnp.zeros((tri_local, local_rows, residues), jnp.bfloat16)
        return (empty, empty)

    left_tri, right_tri = lax.cond(alignment_branch, empty_operands, pair_operands)
    tri_shard_part = lax.all_gather(right_tri, "row", axis=1, tiled=True)
    triangle = lax.optimization_barrier(
        lax.cond(
            alignment_branch,
            lambda: jnp.zeros((tri_local, local_rows, tri_shard_part.shape[1]), jnp.float32),
            lambda: jnp.einsum(
                "cik,cjk->cij", left_tri, tri_shard_part, preferred_element_type=jnp.float32
            ),
        ).astype(jnp.bfloat16)
    )
    tri_float = triangle.astype(jnp.float32)
    summed, squared = lax.psum(
        (jnp.sum(tri_float, axis=0), jnp.sum(tri_float * tri_float, axis=0)), "seq"
    )
    tri_total = tri_local * lax.axis_size("seq")
    average = summed / tri_total
    variance = jnp.maximum(squared / tri_total - average * average, 0.0)
    tri_norm = (
        (tri_float - average) * lax.rsqrt(variance + EPSILON) * triangle_gain[:, None, None]
    ).astype(jnp.bfloat16)
    norm_flat = tri_norm.reshape(tri_local, -1)

    def tri_term(amount):
        return jnp.dot(
            triangle_output_weight, norm_flat, preferred_element_type=jnp.float32
        ).reshape(amount, local_rows, residues)

    def first_term(offset, amount):
        return lax.cond(alignment_branch, lambda: outer_term(amount), lambda: tri_term(amount))

    summed_first = channel_sum(first_term, chan_local)
    outer_increment = (summed_first * (1.0 / seq_total)).astype(jnp.bfloat16)
    gate_values = jax.nn.sigmoid(
        jnp.dot(triangle_gate_weight, tri_flat, preferred_element_type=jnp.float32)
    ).reshape(pair_shape)
    first_update = lax.optimization_barrier(
        (pairwise_input.astype(jnp.float32) + gate_values * summed_first).astype(jnp.bfloat16)
    )
    gathered_next = full_channels(first_update)

    def pair_hidden():
        trans_norm = (
            (layer_normalize(gathered_next.astype(jnp.float32), 0) * transition_gain[:, None, None])
            .astype(jnp.bfloat16)
            .reshape(pair_width, -1)
        )
        return jax.nn.relu(
            jnp.dot(transition_up_weight, trans_norm, preferred_element_type=jnp.float32)
        ).astype(jnp.bfloat16)

    hidden_units = lax.cond(
        alignment_branch,
        lambda: jnp.zeros((trans_local, local_rows * residues), jnp.bfloat16),
        pair_hidden,
    )

    def trans_real(amount):
        return jnp.dot(
            transition_down_weight, hidden_units, preferred_element_type=jnp.float32
        ).reshape(amount, local_rows, residues)

    def trans_term(offset, amount):
        return lax.cond(
            alignment_branch,
            lambda: jnp.zeros((amount, local_rows, residues), jnp.float32),
            lambda: trans_real(amount),
        )

    pair_following = (
        first_update.astype(jnp.float32) + channel_sum(trans_term, chan_local)
    ).astype(jnp.bfloat16)
    half_residues = residues // 2
    halved_width = alignment_channels // 2
    outgoing_product = jnp.where(
        alignment_branch,
        outer_increment[:, :, half_residues:],
        pair_following[:, :, :half_residues],
    )
    incoming = from_partner(outgoing_product, "branch", 0)
    local_half = jnp.where(
        alignment_branch,
        outer_increment[:, :, :half_residues],
        pair_following[:, :, half_residues:],
    )
    pairwise_output = (local_half.astype(jnp.float32) + incoming.astype(jnp.float32)).astype(
        jnp.bfloat16
    )
    mixed_received = shifted(mixed_heads, "branch", 1)
    mixed_applied = jnp.where(alignment_branch, mixed_heads, mixed_received)
    mix_columns = lax.dynamic_slice_in_dim(
        mixing_weight, path_index * halved_width, halved_width, 1
    )
    residual_stream = lax.dynamic_slice_in_dim(
        alignment_input, path_index * halved_width, halved_width, 2
    )
    projected_values = jnp.dot(
        mixed_applied.reshape(-1, latent_heads), mix_columns, preferred_element_type=jnp.float32
    )
    alignment_output = (
        residual_stream.astype(jnp.float32)
        + projected_values.reshape(local_sequences, local_rows, halved_width)
    ).astype(jnp.bfloat16)
    return (alignment_output, pairwise_output)


def solution(mesh):
    return jax.shard_map(
        shards,
        mesh=mesh,
        in_specs=(
            P("seq", "row", None),
            P("seq", "row", None),
            P(),
            P(),
            P(),
            P(),
            P(),
            P(),
            P(),
            P(),
            P(None, "seq", None),
            P("seq", None),
            P("seq"),
            P(None, "seq"),
            P(),
            P("seq", None),
            P(None, "seq"),
        ),
        out_specs=(P("seq", "row", "branch"), P("seq", "row", "branch")),
        check_vma=False,
    )
```

profile of v0, /device:TPU:1, one launch (start us, length us, event | category | flops | bytes accessed | tf_op | source)
XLA Modules:
  0.0 501.4 jit_solution(6505037485555419525)
XLA Ops:
  7.2 12.5 %all_gather.15 = bf16[128,8,256]{2,1,0:T(8,128)(2,1)S(1)} all-gather(bf16[32,8,256]{2,1,0:T(8,128)(2,1)} %param.34), channel_id=1, replica_groups=mesh['branch'=2,'row'=32,'seq'=4] {'seq'}, dimensions={0}, use_global_device_ids=true | all-gather | bytes 655360 | tf_op jit(solution)/shard_map/all_gather | solution.py:27
  19.7 7.5 %conditional.8 = (bf16[8,8,256]{2,1,0:T(8,128)(2,1)S(1)}, bf16[64,8,256]{2,1,0:T(8,128)(2,1)S(1)}, bf16[64,512,8]{1,2,0:T(8,128)(2,1)S(1)}, bf16[64,8,32]{2,1,0:...) conditional(s32[]{:T(128)} %convert_element_type.137, ...), branch_computations={%region_0.0_spmd, %region_3.0_spmd} | conditional | flops 290488832 | bytes 8023212 | solution.py:134
  27.2 1.8 copy.69
  29.9 4.4 conditional.12
  30.0 4.3 convert_bitcast_fusion
  34.3 79.7 %all-gather.8.cloned.1.call-done = bf16[64,32,256]{0,1,2:T(8,128)(2,1)} async-done(((bf16[64,32,8]{0,1,2:T(8,128)(2,1)}), bf16[64,32,256]{0,1,2:T(8,128)(2,1)}) %all-gather.8.cloned.1.call-update) | async-done | bytes 1048592 | tf_op jit(solution)/shard_map/all_gather | solution.py:181
  114.0 86.3 %all-gather.6.cloned.1.call-done = bf16[32,256,256]{2,1,0:T(8,128)(2,1)} async-done(((bf16[32,8,256]{2,1,0:T(8,128)(2,1)}), bf16[32,256,256]{2,1,0:T(8,128)(2,1)}) %all-gather.6.cloned.1.call-update) | async-done | bytes 4194320 | tf_op jit(solution)/shard_map/all_gather | solution.py:215
  200.4 13.1 %all-reduce = (f32[8,256]{1,0:T(8,128)S(1)}, f32[8,256]{1,0:T(8,128)S(1)}) all-reduce(f32[8,256]{1,0:T(8,128)S(1)} %get-tuple-element.213, f32[8,256]{1,0:T(8,128)S(1)} %get-tuple-element.212), channel_id=1, replica_groups=mesh['branch'=2,'row'=32,'seq'=4] {'seq'}, use_global_device_ids=true, to_apply=%region_17.18 | all-reduce | flops 4096 | bytes 32768 | tf_op jit(solution)/shard_map/psum | solution.py:226
  213.7 5.9 %conditional.13 = (f32[128,8,256]{2,1,0:T(8,128)S(1)}) conditional(s32[]{:T(128)} %convert_element_type.137, (bf16[128,32]{0,1:T(8,128)(2,1)S(1)}, bf16[32,8,256]{2,1,0:T(8,128)(2,1)S(1)}) %tuple.142, (bf16[128,8,64,32]{0,2,1,3:T(8,128)(2,1)}, bf16[64,32,256]{0,1,2:T(8,128)(2,1)}) %tuple.77), branch_computations={%region_20.21_spmd, %region_21.22_spmd} | conditional | flops 1073741824 | bytes 8388616 | solution.py:243
  213.7 5.3 %fusion.55 = f32[128,8,256]{2,0,1:T(8,128)S(1)} fusion(bf16[128,8,64,32]{0,2,1,3:T(8,128)(2,1)} %get-tuple-element.207, bf16[64,32,256,1]{0,1,2,3:T(8,128)(2,1)} %bitcast.139), kind=kOutput, calls=%fused_computation.72 | convolution fusion | flops 1073741824 | bytes 6291456 | tf_op jit(solution)/shard_map/cond/branch_1_fun/dot_general | solution.py:193
  221.1 21.9 %reduce-scatter.3.cloned.1.call-done = f32[32,8,256]{2,1,0:T(8,128)} async-done(((f32[128,8,256]{2,1,0:T(8,128)}), f32[32,8,256]{2,1,0:T(8,128)}) %reduce-scatter.3.cloned.1.call-update) | async-done | bytes 262160 | tf_op jit(solution)/shard_map/reduce_scatter | solution.py:31
  243.0 1.6 multiply_convert_fusion
  244.7 10.7 %all_gather.19 = bf16[128,8,256]{2,1,0:T(8,128)(2,1)S(1)} all-gather(bf16[32,8,256]{2,1,0:T(8,128)(2,1)S(1)} %get-tuple-element.225), channel_id=1, replica_groups=mesh['branch'=2,'row'=32,'seq'=4] {'seq'}, dimensions={0}, use_global_device_ids=true | all-gather | bytes 655360 | tf_op jit(solution)/shard_map/all_gather | solution.py:27
  259.4 26.8 %reduce-scatter.5.cloned.1.call-done = f32[32,8,256]{2,1,0:T(8,128)} async-done(((f32[128,8,256]{2,1,0:T(8,128)}), f32[32,8,256]{2,1,0:T(8,128)}) %reduce-scatter.5.cloned.1.call-update) | async-done | bytes 262160 | tf_op jit(solution)/shard_map/reduce_scatter | solution.py:31
  289.0 138.7 %all-gather.4.cloned.1.call-done = bf16[64,512,256]{1,0,2:T(8,128)(2,1)} async-done(((bf16[64,512,8]{1,0,2:T(8,128)(2,1)}), bf16[64,512,256]{1,0,2:T(8,128)(2,1)}) %all-gather.4.cloned.1.call-update) | async-done | bytes 16777232 | tf_op jit(solution)/shard_map/all_gather | solution.py:174
  427.7 48.7 %conditional.9 = (f32[64,8,8]{2,1,0:T(8,128)S(1)}, f32[64,8,8,32]{3,2,1,0:T(8,128)}) conditional(s32[]{:T(128)} %convert_element_type.137, () %tuple.68, (bf16[64,512,256]{1,0,2:T(8,128)(2,1)}, bf16[64,8,8,32]{0,3,1,2:T(8,128)(2,1)S(1)}, bf16[8,8,256]{2,1,0:T(8,128)(2,1)S(1)}) %tuple.138), branch_computations={%region_6.0_spmd, %region_7.0_spmd} | conditional | flops 142618624 | bytes 131727400 | solution.py:175
  427.7 24.9 %copy.62 = bf16[64,512,256]{2,1,0:T(8,128)(2,1)} copy(bf16[64,512,256]{1,0,2:T(8,128)(2,1)} %get-tuple-element.200) | data formatting | bytes 33554432 | tf_op jit(solution)/shard_map
  452.6 11.6 %fusion.79 = (bf16[64,256,256]{2,1,0:T(8,128)(2,1)}, bf16[64,256,256]{2,1,0:T(8,128)(2,1)}) fusion(bf16[64,512,256]{2,1,0:T(8,128)(2,1)} %copy.62), kind=kLoop, calls=%fused_computation.116 | loop fusion | bytes 33554432 | tf_op jit(solution)/shard_map/cond/branch_1_fun/slice | solution.py:148
  464.2 1.6 copy.63
  465.8 4.8 add_reduce_fusion
  471.6 3.5 fusion.37
  476.4 1.9 divide_bitcast_fusion
  482.4 1.6 add_convert_fusion.1
  483.9 9.7 %collective-permute-done.1 = bf16[64,8,256]{0,2,1:T(8,128)(2,1)S(1)} collective-permute-done((bf16[64,8,256]{0,2,1:T(8,128)(2,1)S(1)}, bf16[64,8,256]{0,2,1:T(8,128)(2,1)S(1)}, u32[]{:S(2)}, u32[]{:S(2)}) %collective-permute-start.1) | collective-permute-done | bytes 262176 | tf_op jit(solution)/shard_map/ppermute | solution.py:12
  (100 shorter events, 24.9 us)
Async XLA Ops:
  7.2 486.8 %copy-start = (bf16[256,256]{1,0:T(8,128)(2,1)S(1)}, bf16[256,256]{1,0:T(8,128)(2,1)}, u32[]{:S(2)}) copy-start(bf16[256,256]{1,0:T(8,128)(2,1)} %param.38) | copy-start | bytes 393220
  7.2 106.9 %all-gather.8.cloned.1.call-start = ((), (), s32[]{:S(2)}) async-start(), calls=%async_computation.4 | async-start | bytes 2162688 | tf_op jit(solution)/shard_map/all_gather | solution.py:181
  19.7 9.3 %copy-start.11 = (bf16[4,32,128]{2,1,0:T(8,128)(2,1)S(1)}, bf16[4,32,128]{2,1,0:T(8,128)(2,1)}, u32[]{:S(2)}) copy-start(bf16[4,32,128]{2,1,0:T(8,128)(2,1)} %param.43) | copy-start | bytes 98308
  19.7 5.2 %copy-start.6 = (bf16[64,8,256]{2,1,0:T(8,128)(2,1)S(1)}, bf16[64,8,256]{2,1,0:T(8,128)(2,1)}, u32[]{:S(2)}) copy-start(bf16[64,8,256]{2,1,0:T(8,128)(2,1)} %get-tuple-element.73) | copy-start | bytes 786436 | tf_op jit(solution)/shard_map/cond
  19.7 5.2 %copy-start.19 = (f32[256]{0:T(256)S(1)}, f32[256]{0:T(256)}, u32[]{:S(2)}) copy-start(f32[256]{0:T(256)} %get-tuple-element.128) | copy-start | bytes 3076 | tf_op jit(solution)/shard_map/cond
  22.1 3.6 copy-start.17
  29.0 171.4 %all-gather.6.cloned.1.call-start = ((), (), s32[]{:S(2)}) async-start(), calls=%async_computation.3 | async-start | bytes 4325376 | tf_op jit(solution)/shard_map/all_gather | solution.py:215
  29.8 213.2 %reduce-scatter.3.cloned.1.call-start = ((), (), s32[]{:S(2)}) async-start(), calls=%async_computation.5 | async-start | bytes 1310720 | tf_op jit(solution)/shard_map/reduce_scatter | solution.py:31
  34.3 179.2 %copy-start.15 = (f32[32]{0:T(128)S(1)}, f32[32]{0:T(128)}, u32[]{:S(2)}) copy-start(f32[32]{0:T(128)} %param.45) | copy-start | bytes 388
  34.3 179.3 %copy-start.14 = (bf16[128,32]{0,1:T(8,128)(2,1)S(1)}, bf16[128,32]{0,1:T(8,128)(2,1)}, u32[]{:S(2)}) copy-start(bf16[128,32]{0,1:T(8,128)(2,1)} %param.46) | copy-start | bytes 24580
  213.6 7.1 %copy-start.18 = (bf16[32,128]{1,0:T(8,128)(2,1)S(1)}, bf16[32,128]{1,0:T(8,128)(2,1)}, u32[]{:S(2)}) copy-start(bf16[32,128]{1,0:T(8,128)(2,1)} %param.44) | copy-start | bytes 24580
  213.7 29.4 %copy-start.7 = (bf16[32,8,256]{2,1,0:T(8,128)(2,1)S(1)}, bf16[32,8,256]{2,1,0:T(8,128)(2,1)}, u32[]{:S(2)}) copy-start(bf16[32,8,256]{2,1,0:T(8,128)(2,1)} %param.34) | copy-start | bytes 393220
  219.6 35.8 %copy-start.12 = (bf16[128,128]{1,0:T(8,128)(2,1)S(1)}, bf16[128,128]{1,0:T(8,128)(2,1)}, u32[]{:S(2)}) copy-start(bf16[128,128]{1,0:T(8,128)(2,1)} %param.48) | copy-start | bytes 98308
  219.6 35.8 %copy-start.16 = (f32[128]{0:T(128)S(1)}, f32[128]{0:T(128)}, u32[]{:S(2)}) copy-start(f32[128]{0:T(128)} %param.47) | copy-start | bytes 1540
  220.7 34.9 %copy-start.13 = (bf16[128,128]{1,0:T(8,128)(2,1)S(1)}, bf16[128,128]{1,0:T(8,128)(2,1)}, u32[]{:S(2)}) copy-start(bf16[128,128]{1,0:T(8,128)(2,1)} %param.49) | copy-start | bytes 98308
  220.7 65.5 %reduce-scatter.5.cloned.1.call-start = ((), (), s32[]{:S(2)}) async-start(), calls=%async_computation.6 | async-start | bytes 1310720 | tf_op jit(solution)/shard_map/reduce_scatter | solution.py:31
  255.6 31.6 %copy-start.8 = (bf16[32,8,256]{2,1,0:T(8,128)(2,1)S(1)}, bf16[32,8,256]{2,1,0:T(8,128)(2,1)}, u32[]{:S(2)}) copy-start(bf16[32,8,256]{2,1,0:T(8,128)(2,1)} %get-tuple-element.224) | copy-start | bytes 393220
  256.7 171.0 %all-gather.4.cloned.1.call-start = ((), (), s32[]{:S(2)}) async-start(), calls=%async_computation.2 | async-start | bytes 17301504 | tf_op jit(solution)/shard_map/all_gather | solution.py:174
  257.8 31.2 %collective-permute-start = (bf16[8,8,256]{2,1,0:T(8,128)(2,1)S(1)}, bf16[8,8,256]{2,1,0:T(8,128)(2,1)S(1)}, u32[]{:S(2)}, u32[]{:S(2)}) collective-permute-start(bf16[8,8,256]{2,1,0:T(8,128)(2,1)S(1)} %get-tuple-element.112), channel_id=1, source_target_pairs={{128,0},{129,1},{130,2},{131,3},{132,4},{133,5},{134,6},{135,7},{1... | collective-permute-start | bytes 98312 | tf_op jit(solution)/shard_map/ppermute | solution.py:12
  287.1 140.6 %copy-start.10 = (bf16[32,8,256]{2,1,0:T(8,128)(2,1)}, bf16[32,8,256]{2,1,0:T(8,128)(2,1)S(1)}, u32[]{:S(2)}) copy-start(bf16[32,8,256]{2,1,0:T(8,128)(2,1)S(1)} %add_convert_fusion) | copy-start | bytes 393220
  287.8 194.6 %collective-permute-start.2 = (bf16[32,8,128]{2,1,0:T(8,128)(2,1)}, bf16[32,8,128]{2,1,0:T(8,128)(2,1)}, u32[]{:S(2)}, u32[]{:S(2)}) collective-permute-start(bf16[32,8,128]{2,1,0:T(8,128)(2,1)} %slice_select_fusion), channel_id=1, source_target_pairs={{0,128},{128,0},{1,129},{129,1},{2,130},{130,2},{3,131},{131,3},{4... | collective-permute-start | bytes 196616 | tf_op jit(solution)/shard_map/ppermute | solution.py:16
  465.8 5.8 %copy-start.1 = (bf16[64,256,256]{2,1,0:T(8,128)(2,1)S(1)}, bf16[64,256,256]{2,1,0:T(8,128)(2,1)}, u32[]{:S(2)}) copy-start(bf16[64,256,256]{2,1,0:T(8,128)(2,1)} %get-tuple-element.218) | copy-start | bytes 25165828 | tf_op jit(solution)/shard_map/cond
  478.4 15.5 %copy-start.5 = (bf16[64,8,256]{2,1,0:T(8,128)(2,1)S(1)}, bf16[64,8,256]{2,1,0:T(8,128)(2,1)}, u32[]{:S(2)}) copy-start(bf16[64,8,256]{2,1,0:T(8,128)(2,1)} %param.33) | copy-start | bytes 786436
  481.0 12.6 %collective-permute-start.1 = (bf16[64,8,256]{0,2,1:T(8,128)(2,1)S(1)}, bf16[64,8,256]{0,2,1:T(8,128)(2,1)S(1)}, u32[]{:S(2)}, u32[]{:S(2)}) collective-permute-start(bf16[64,8,256]{0,2,1:T(8,128)(2,1)S(1)} %fusion.69), channel_id=1, source_target_pairs={{0,128},{1,129},{2,130},{3,131},{4,132},{5,133},{6,134},{7,135},{8... | collective-permute-start | bytes 786440 | tf_op jit(solution)/shard_map/ppermute | solution.py:12
  (5 other events, 8.9 us)
Sparse Core Ops, SparseCore 0:
  29.1 84.8 all-gather.7
  117.2 83.1 all-gather.5
  220.8 22.1 reduce-scatter.2
  256.8 29.2 reduce-scatter.4
  288.8 138.8 all-gather.3
where the time goes:
time: 503 us; the launch traced here: 501 us
  waiting for transfers between devices  363 us (72%)
  local copies, waits for them, and re-layouts  49 us (10%)
  blocking collectives  36.3 us (7%)
  matrix products  22.3 us (4%)
  between operations  14.1 us (3%)
  other arithmetic  12.1 us (2%)
    all_gather x1, waiting for transfers between devices, shards(): shard_part = lax.all_gather(key_values, 'row', axis=2, tiled=True)  139 us
    all_gather x1, waiting for transfers between devices, shards(): tri_shard_part = lax.all_gather(right_tri, 'row', axis=1, tiled=True)  86.3 us
    all_gather x1, waiting for transfers between devices, shards(): right_full = lax.all_gather(right_cols, 'row', axis=2, tiled=True)  79.7 us
    reduce_scatter x2, waiting for transfers between devices, channel_sum(): lax.psum_scatter(term(jnp.int32(0), kept_rows * lax.axis_size('seq')), 's...  48.7 us
    another operation x10, local copies, waits for them, and re-layouts  27.9 us
    all_gather x2, blocking collectives, full_channels(): return lax.all_gather(values, 'seq', axis=0, tiled=True)  23.2 us
    psum x1, blocking collectives, shards(): lax.psum((jnp.sum(tri_float, axis=0), jnp.sum(tri_float * tri_float, axis...  13.1 us
    slice x1, local copies, waits for them, and re-layouts, fold_real(): shard_part[:, latent_heads:]  11.6 us
  transfers between devices with their start and end apart: 8, of which 6 were waited for; matrix products, arithmetic and copies ran while one was open for 12% of the time, Pallas kernels for 0%

commit v1 on v0

v1 whole, which is shorter than its diff:
```python
import jax
import jax.numpy as jnp
from jax import lax
from jax.sharding import PartitionSpec as P

EPSILON = 1e-05
BF = jnp.bfloat16
F32 = jnp.float32


def layer_normalize(values, axis):
    average = jnp.mean(values, axis=axis, keepdims=True)
    centred = values - average
    spread = jnp.mean(centred * centred, axis=axis, keepdims=True)
    return centred * lax.rsqrt(spread + EPSILON)


def mm(a, b):
    return jnp.dot(a, b, preferred_element_type=F32)


def shards(
    alignment_input,
    pairwise_input,
    alignment_gain,
    product_gain,
    attention_weight,
    mixing_weight,
    outer_input_weight,
    outer_output_weight,
    bias_matrix,
    pairwise_gain,
    triangle_input_weight,
    triangle_gate_weight,
    triangle_gain,
    triangle_output_weight,
    transition_gain,
    transition_up_weight,
    transition_down_weight,
):
    sl, il, mw = alignment_input.shape
    cl, _, res = pairwise_input.shape
    pw, heads = bias_matrix.shape
    width = mixing_weight.shape[0]
    hd = width // heads
    pc = outer_input_weight.shape[2]
    rows = lax.axis_size("row")
    nq = lax.axis_size("seq")
    nb = lax.axis_size("branch")
    so = sl // rows
    hb = heads // nb
    wb = width // nb
    half = il // nb
    b = lax.axis_index("branch")
    q = lax.axis_index("seq")

    full = lax.all_gather(pairwise_input, "seq", axis=0, tiled=True)
    packed = jnp.concatenate(
        [
            triangle_gate_weight,
            triangle_output_weight.T,
            transition_up_weight,
            transition_down_weight.T,
        ],
        axis=0,
    )
    packed = lax.all_gather(packed, "seq", axis=0)
    tg_full = lax.all_gather(triangle_gain, "seq", axis=0, tiled=True)
    tl = transition_up_weight.shape[0]
    gate_w = packed[:, :cl].reshape(pw, pw)
    out_wt = packed[:, cl : 2 * cl].reshape(pw, pw)
    up_w = packed[:, 2 * cl : 2 * cl + tl].reshape(nq * tl, pw)
    down_wt = packed[:, 2 * cl + tl :].reshape(nq * tl, pw)

    mine = lax.all_to_all(alignment_input, "row", split_axis=0, concat_axis=1, tiled=True)

    unit = layer_normalize(full.astype(F32), 0)
    plain = unit.astype(BF).reshape(pw, -1)
    tri_input = (unit * pairwise_gain[:, None, None]).astype(BF)
    bias_all = lax.dot_general(
        bias_matrix, plain, (((0,), (0,)), ((), ())), preferred_element_type=F32
    ).astype(BF)
    bias_own = lax.dynamic_slice_in_dim(bias_all, hb * b + q, 1, 0).reshape(il, res)
    tri_flat = tri_input.reshape(pw, -1)
    tri_half = lax.dynamic_slice_in_dim(tri_input, half * b, half, 1).reshape(pw, -1)
    lin_l = mm(triangle_input_weight[:2].reshape(2 * cl, pw), tri_half).reshape(2, cl, half, res)
    lin_r = mm(triangle_input_weight[2:].reshape(2 * cl, pw), tri_flat).reshape(2, cl, il, res)
    left_tri = (lin_l[0] * jax.nn.sigmoid(lin_l[1])).astype(BF)
    right_tri = (lin_r[0] * jax.nn.sigmoid(lin_r[1])).astype(BF)
    sent = jnp.concatenate([left_tri, right_tri], axis=1)
    got = lax.all_to_all(sent, "row", split_axis=0, concat_axis=0, tiled=True)
    tri_l = got[:, :half].reshape(rows * half, res)
    tri_r = got[:, half:].reshape(rows * il, res)
    triangle = lax.dot_general(
        tri_l, tri_r, (((1,), (1,)), ((), ())), preferred_element_type=F32
    ).astype(BF)

    bias = lax.all_gather(bias_own, "row", axis=0, tiled=True)
    bias = lax.all_gather(bias, "seq", axis=0)
    stat = layer_normalize(mine.astype(F32), 2)
    normed = (stat * alignment_gain).astype(BF).reshape(so * res, mw)
    weights = lax.dynamic_slice_in_dim(attention_weight, wb * b, wb, 2)
    proj = mm(normed, weights.reshape(mw, 4 * wb)).reshape(so, res, 4, hb, hd)
    query = (proj[:, :, 0] * hd ** (-0.5)).astype(BF)
    keys = proj[:, :, 1].astype(BF)
    values = proj[:, :, 2].astype(BF)
    gate = jax.nn.sigmoid(proj[:, :, 3]).astype(BF)
    scores = jnp.einsum("sihd,sjhd->shij", query, keys, preferred_element_type=F32) + bias.astype(
        F32
    )
    top = jnp.max(scores, axis=3, keepdims=True)
    expo = jnp.exp(scores - top)
    totals = jnp.sum(expo, axis=3)
    weighted = jnp.einsum("shij,sjhd->sihd", expo.astype(BF), values, preferred_element_type=F32)
    mixed = (
        gate.astype(F32) * (weighted / totals.transpose(0, 2, 1)[..., None])
    ).astype(BF)
    mixed = mixed.reshape(so, res, wb)
    mixed = lax.all_to_all(mixed, "row", split_axis=1, concat_axis=0, tiled=True)
    other = lax.ppermute(mixed, "branch", [(i, i ^ 1) for i in range(nb)])
    cols = lax.dynamic_slice_in_dim(mixing_weight, wb * b, wb, 1)
    w_own = lax.dynamic_slice_in_dim(cols, wb * b, wb, 0)
    w_other = lax.dynamic_slice_in_dim(cols, wb * (1 - b), wb, 0)
    residual = lax.dynamic_slice_in_dim(alignment_input, wb * b, wb, 2)
    projected = mm(mixed.reshape(-1, wb), w_own) + mm(other.reshape(-1, wb), w_other)
    alignment_output = (residual.astype(F32) + projected.reshape(sl, il, wb)).astype(BF)

    local = layer_normalize(alignment_input.astype(F32), 2)
    local = (local * product_gain).astype(BF).reshape(-1, mw)
    left = mm(local, outer_input_weight[:, 0]).astype(BF).reshape(sl, il * pc)
    outer_norm = (stat * product_gain).astype(BF)
    right = jnp.einsum(
        "sjm,md->sdj", outer_norm, outer_input_weight[:, 1], preferred_element_type=F32
    ).astype(BF)
    right = lax.dynamic_slice_in_dim(right, (res // nb) * b, res // nb, 2)
    right = lax.all_gather(right, "row", axis=0, tiled=True)
    prod = lax.dot_general(
        left, right.reshape(sl, -1), (((0,), (0,)), ((), ())), preferred_element_type=F32
    ).astype(BF)
    prod = prod.reshape(il, pc, pc, res // nb).transpose(0, 2, 1, 3).reshape(il, pc * pc, res // nb)
    w_outer = outer_output_weight.transpose(1, 0, 2).reshape(pc * pc, pw)
    outer = jnp.einsum("ikj,ko->oij", prod, w_outer, preferred_element_type=F32)
    outer = lax.psum_scatter(outer, "seq", scatter_dimension=0, tiled=True)
    outer_update = (outer * (1.0 / (sl * nq))).astype(BF)

    back = lax.all_to_all(
        triangle.reshape(rows, half, res), "row", split_axis=0, concat_axis=0, tiled=True
    )
    row_tri = lax.all_to_all(back, "seq", split_axis=1, concat_axis=0, tiled=True).reshape(pw, res)
    pick = half * b + q
    pair_row = lax.dynamic_slice_in_dim(full, pick, 1, 1).reshape(pw, res).astype(F32)
    tri_row = lax.dynamic_slice_in_dim(tri_input, pick, 1, 1).reshape(pw, res)
    tri_norm = (layer_normalize(row_tri.astype(F32), 0) * tg_full[:, None]).astype(BF)
    tri_out = lax.dot_general(
        out_wt, tri_norm, (((0,), (0,)), ((), ())), preferred_element_type=F32
    )
    first = (pair_row + jax.nn.sigmoid(mm(gate_w, tri_row)) * tri_out).astype(BF).astype(F32)
    trans = (layer_normalize(first, 0) * transition_gain[:, None]).astype(BF)
    hidden = jax.nn.relu(mm(up_w, trans)).astype(BF)
    pair_next = (
        first
        + lax.dot_general(down_wt, hidden, (((0,), (0,)), ((), ())), preferred_element_type=F32)
    ).astype(BF)
    parts = pair_next.reshape(nq, cl, nb, res // nb).transpose(2, 0, 1, 3)
    parts = parts.reshape(nb * nq, cl, res // nb)
    parts = lax.all_to_all(parts, ("branch", "seq"), split_axis=0, concat_axis=0, tiled=True)
    parts = parts.transpose(1, 0, 2)
    pairwise_output = (parts.astype(F32) + outer_update.astype(F32)).astype(BF)
    return (alignment_output, pairwise_output)


def solution(mesh):
    return jax.shard_map(
        shards,
        mesh=mesh,
        in_specs=(
            P("seq", "row", None),
            P("seq", "row", None),
            P(),
            P(),
            P(),
            P(),
            P(),
            P(),
            P(),
            P(),
            P(None, "seq", None),
            P("seq", None),
            P("seq"),
            P(None, "seq"),
            P(),
            P("seq", None),
            P(None, "seq"),
        ),
        out_specs=(P("seq", "row", "branch"), P("seq", "row", "branch")),
        check_vma=False,
    )
```

time: 503 us -> 238 us (0.47)
  waiting for transfers between devices: 363 us -> 12.3 us
  blocking collectives: 36.3 us -> 132 us
  starting transfers between devices: 4.04 us -> 46 us
  local copies, waits for them, and re-layouts: 49 us -> 14.9 us
  matrix products: 22.3 us -> 8.93 us
    all_gather x3 -> x0, waiting for transfers between devices: 305 us -> none  [the longest x1 139 us: shards(): shard_part = lax.all_gather(key_values, 'row', axis=2, tiled=True)]
    all_gather x2 -> x5, blocking collectives: 23.2 us -> 122 us  [the longest x1 44.8 us: shards(): right = lax.all_gather(right, 'row', axis=0, tiled=True)]
    reduce_scatter x2 -> x1, waiting for transfers between devices: 48.7 us -> 0.01 us  [shards(): outer = lax.psum_scatter(outer, 'seq', scatter_dimension=0, tiled=True)]
    all_to_all x0 -> x6, starting transfers between devices: none -> 44.4 us  [the longest x1 13.6 us: shards(): got = lax.all_to_all(sent, 'row', split_axis=0, concat_axis=0, tiled=True)]
    another operation x10 -> x1, local copies, waits for them, and re-layouts: 27.9 us -> 0.06 us
    dot_general x11 -> x16, matrix products: 22.3 us -> 8.93 us  [the longest x7 4.36 us: mm(): return jnp.dot(a, b, preferred_element_type=F32)]
    psum x1 -> x0, blocking collectives: 13.1 us -> none  [shards(): lax.psum((jnp.sum(tri_float, axis=0), jnp.sum(tri_float * tri_float, axis...]
    unnamed x0 -> x1, blocking collectives: none -> 9.69 us
  transfers between devices with their start and end apart: 8 -> 8, of which waited for: 6 -> 2; matrix products, arithmetic and copies ran while one was open for 12% -> 10% of each run, Pallas kernels for 0% -> 0%
where the time goes in v1:
time: 238 us; the launch traced here: 237 us
  blocking collectives  132 us (55%)
  starting transfers between devices  46 us (19%)
  between operations  15.4 us (6%)
  local copies, waits for them, and re-layouts  14.9 us (6%)
  waiting for transfers between devices  12.3 us (5%)
  matrix products  8.93 us (4%)
  other arithmetic  7.29 us (3%)
    all_gather x1, blocking collectives, shards(): right = lax.all_gather(right, 'row', axis=0, tiled=True)  44.8 us
    all_gather x1, blocking collectives, shards(): bias = lax.all_gather(bias_own, 'row', axis=0, tiled=True)  42.3 us
    all_to_all x1, starting transfers between devices, shards(): got = lax.all_to_all(sent, 'row', split_axis=0, concat_axis=0, tiled=True)  13.6 us
    all_gather x1, blocking collectives, shards(): full = lax.all_gather(pairwise_input, 'seq', axis=0, tiled=True)  12.3 us
    all_to_all x1, starting transfers between devices, shards(): lax.all_to_all(alignment_input, 'row', split_axis=0, concat_axis=1, tiled...  11.7 us
    all_gather x1, blocking collectives, shards(): packed = lax.all_gather(packed, 'seq', axis=0)  11.5 us
    all_gather x1, blocking collectives, shards(): bias = lax.all_gather(bias, 'seq', axis=0)  11.4 us
    unnamed x1, blocking collectives  9.69 us
  transfers between devices with their start and end apart: 8, of which 2 were waited for; matrix products, arithmetic and copies ran while one was open for 10% of the time, Pallas kernels for 0%

profile of v1, /device:TPU:1, one launch (start us, length us, event | category | flops | bytes accessed | tf_op | source)
XLA Modules:
  0.0 236.7 jit_solution(16625298647050164742)
XLA Ops:
  8.2 12.3 %all_gather.24 = bf16[128,8,256]{2,0,1:T(8,128)(2,1)S(1)} all-gather(bf16[32,8,256]{2,0,1:T(8,128)(2,1)S(1)} %copy.52), channel_id=1, replica_groups=mesh['branch'=2,'row'=32,'seq'=4] {'seq'}, dimensions={0}, use_global_device_ids=true | all-gather | bytes 655360 | tf_op jit(solution)/shard_map/all_gather | solution.py:57
  23.7 13.6 %all-to-all-start.2 = ((bf16[32,12,256]{2,1,0:T(8,128)(2,1)}), bf16[32,12,256]{2,1,0:T(8,128)(2,1)S(1)}, u32[]{:S(2)}, u32[]{:S(2)}) async-start(bf16[32,12,256]{2,1,0:T(8,128)(2,1)} %pad_maximum_fusion), calls=%async_computation.2 | async-start | bytes 524288 | tf_op jit(solution)/shard_map/all_to_all | solution.py:91
  37.4 1.1 convert_reduce_fusion.1
  38.5 1.2 fusion.33
  40.4 42.3 %all_gather.25 = bf16[256,256]{1,0:T(8,128)(2,1)S(1)} all-gather(bf16[8,256]{1,0:T(8,128)(2,1)S(1)} %reshape.275), channel_id=1, replica_groups=mesh['branch'=2,'row'=32,'seq'=4] {'row'}, dimensions={0}, use_global_device_ids=true | all-gather | bytes 135168 | tf_op jit(solution)/shard_map/all_gather | solution.py:98
  82.6 11.4 %all-gather = bf16[1024,256]{1,0:T(8,128)(2,1)S(1)} all-gather(bf16[256,256]{1,0:T(8,128)(2,1)S(1)} %all_gather.25), channel_id=2, replica_groups=mesh['branch'=2,'row'=32,'seq'=4] {'seq'}, dimensions={0}, use_global_device_ids=true | all-gather | bytes 655360 | tf_op jit(solution)/shard_map/all_gather | solution.py:99
  94.1 1.3 convolution_convert_fusion.2
  96.3 6.5 %all-to-all-start.3 = ((bf16[32,4,256]{2,1,0:T(4,128)(2,1)}), bf16[32,4,256]{2,1,0:T(4,128)(2,1)S(1)}, u32[]{:S(2)}, u32[]{:S(2)}) async-start(bf16[32,4,256]{2,1,0:T(4,128)(2,1)} %reshape.289), calls=%async_computation.3 | async-start | bytes 131072 | tf_op jit(solution)/shard_map/all_to_all | solution.py:146
  102.8 11.5 %all-gather.1 = bf16[1280,128]{1,0:T(8,128)(2,1)} all-gather(bf16[320,128]{1,0:T(8,128)(2,1)S(1)} %pad_maximum_fusion.1), channel_id=3, replica_groups=mesh['branch'=2,'row'=32,'seq'=4] {'seq'}, dimensions={0}, use_global_device_ids=true | all-gather | bytes 409600 | tf_op jit(solution)/shard_map/all_gather | solution.py:67
  114.3 11.7 %all-to-all-start = ((bf16[64,8,256]{2,1,0:T(8,128)(2,1)}), bf16[64,8,256]{2,1,0:T(8,128)(2,1)S(1)}, u32[]{:S(2)}, u32[]{:S(2)}) async-start(bf16[64,8,256]{2,1,0:T(8,128)(2,1)} %param.17), calls=%async_computation | async-start | bytes 524288 | tf_op jit(solution)/shard_map/all_to_all | solution.py:75
  128.3 9.7 %all-reduce = f32[128]{0:T(128)S(1)} all-reduce(f32[128]{0:T(128)S(1)} %dynamic-update-slice), channel_id=1, replica_groups=mesh['branch'=2,'row'=32,'seq'=4] {'seq'}, use_global_device_ids=true, to_apply=%add | all-reduce | flops 128 | bytes 1024
  138.6 1.1 copy.73
  139.7 1.4 fusion.110
  141.1 1.7 fusion.109
  143.4 3.3 %all-to-all-start.4 = ((bf16[32,4,256]{2,0,1:T(8,128)(2,1)}), bf16[32,4,256]{2,0,1:T(8,128)(2,1)S(1)}, u32[]{:S(2)}, u32[]{:S(2)}) async-start(bf16[32,4,256]{2,0,1:T(8,128)(2,1)} %copy.63), calls=%async_computation.4 | async-start | bytes 131072 | tf_op jit(solution)/shard_map/all_to_all | solution.py:149
  148.4 44.8 %all_gather.31 = bf16[64,32,128]{2,1,0:T(8,128)(2,1)S(1)} all-gather(bf16[2,32,128]{2,1,0:T(8,128)(2,1)S(1)} %fusion.100), channel_id=1, replica_groups=mesh['branch'=2,'row'=32,'seq'=4] {'row'}, dimensions={0}, use_global_device_ids=true | all-gather | bytes 540672 | tf_op jit(solution)/shard_map/all_gather | solution.py:136
  194.9 1.6 fusion.6
  196.4 2.0 copy.67
  201.1 4.8 %all-to-all-start.1 = ((bf16[2,256,128]{2,0,1:T(2,128)(2,1)}), bf16[2,256,128]{2,0,1:T(2,128)(2,1)S(1)}, u32[]{:S(2)}, u32[]{:S(2)}) async-start(bf16[2,256,128]{2,0,1:T(2,128)(2,1)} %copy.56), calls=%async_computation.1 | async-start | bytes 262144 | tf_op jit(solution)/shard_map/all_to_all | solution.py:119
  207.8 8.9 %all-to-all-done.1 = bf16[2,256,128]{2,0,1:T(2,128)(2,1)S(1)} async-done(((bf16[2,256,128]{2,0,1:T(2,128)(2,1)}), bf16[2,256,128]{2,0,1:T(2,128)(2,1)S(1)}, u32[]{:S(2)}, u32[]{:S(2)}) %all-to-all-start.1) | async-done | bytes 131104 | tf_op jit(solution)/shard_map/all_to_all | solution.py:119
  216.6 4.5 %all-to-all-start.5 = ((bf16[8,32,128]{2,1,0:T(8,128)(2,1)}), bf16[8,32,128]{2,1,0:T(8,128)(2,1)S(1)}, u32[]{:S(2)}, u32[]{:S(2)}) async-start(bf16[8,32,128]{2,1,0:T(8,128)(2,1)} %bitcast.47), calls=%async_computation.5 | async-start | bytes 131072 | tf_op jit(solution)/shard_map/all_to_all | solution.py:166
  221.2 1.5 collective-permute-start
  223.0 3.4 %collective-permute-done = bf16[64,8,128]{2,1,0:T(8,128)(2,1)S(1)} collective-permute-done((bf16[64,8,128]{2,1,0:T(8,128)(2,1)S(1)}, bf16[64,8,128]{2,1,0:T(8,128)(2,1)S(1)}, u32[]{:S(2)}, u32[]{:S(2)}) %collective-permute-start) | collective-permute-done | bytes 131104 | tf_op jit(solution)/shard_map/ppermute | solution.py:120
  226.4 1.8 fusion.15
  (118 shorter events, 18.0 us)
Async XLA Ops:
  7.2 118.9 %copy-start = (bf16[256,4,256]{2,1,0:T(4,128)(2,1)S(1)}, bf16[256,4,256]{2,1,0:T(4,128)(2,1)}, u32[]{:S(2)}) copy-start(bf16[256,4,256]{2,1,0:T(4,128)(2,1)} %param.21) | copy-start | bytes 1572868
  22.1 15.2 %copy-start.6 = (bf16[128,128]{1,0:T(8,128)(2,1)S(1)}, bf16[128,128]{1,0:T(8,128)(2,1)}, u32[]{:S(2)}) copy-start(bf16[128,128]{1,0:T(8,128)(2,1)} %param.33) | copy-start | bytes 98308
  22.7 17.3 %copy-start.11 = (bf16[128,8]{0,1:T(8,128)(2,1)S(1)}, bf16[128,8]{0,1:T(8,128)(2,1)}, u32[]{:S(2)}) copy-start(bf16[128,8]{0,1:T(8,128)(2,1)} %param.25) | copy-start | bytes 6148
  22.9 71.2 %copy-start.12 = (f32[256]{0:T(256)S(1)}, f32[256]{0:T(256)}, u32[]{:S(2)}) copy-start(f32[256]{0:T(256)} %param.20) | copy-start | bytes 3076
  22.9 71.2 %copy-start.15 = (bf16[256,2,32]{0,2,1:T(8,128)(2,1)S(1)}, bf16[256,2,32]{0,2,1:T(8,128)(2,1)}, u32[]{:S(2)}) copy-start(bf16[256,2,32]{0,2,1:T(8,128)(2,1)} %param.23) | copy-start | bytes 98308
  23.7 71.7 %all-to-all-start.2 = ((bf16[32,12,256]{2,1,0:T(8,128)(2,1)}), bf16[32,12,256]{2,1,0:T(8,128)(2,1)S(1)}, u32[]{:S(2)}, u32[]{:S(2)}) async-start(bf16[32,12,256]{2,1,0:T(8,128)(2,1)} %pad_maximum_fusion), calls=%async_computation.2 | async-start | bytes 524288 | tf_op jit(solution)/shard_map/all_to_all | solution.py:91
  39.7 63.0 %copy-start.4 = (bf16[128,128]{1,0:T(8,128)(2,1)S(1)}, bf16[128,128]{1,0:T(8,128)(2,1)}, u32[]{:S(2)}) copy-start(bf16[128,128]{1,0:T(8,128)(2,1)} %param.32) | copy-start | bytes 98308
  39.7 63.0 %copy-start.9 = (bf16[128,32]{0,1:T(8,128)(2,1)S(1)}, bf16[128,32]{0,1:T(8,128)(2,1)}, u32[]{:S(2)}) copy-start(bf16[128,32]{0,1:T(8,128)(2,1)} %param.30) | copy-start | bytes 24580
  39.8 63.0 %copy-start.10 = (bf16[32,128]{1,0:T(8,128)(2,1)S(1)}, bf16[32,128]{1,0:T(8,128)(2,1)}, u32[]{:S(2)}) copy-start(bf16[32,128]{1,0:T(8,128)(2,1)} %param.28) | copy-start | bytes 24580
  82.6 44.2 %copy-start.19 = (u32[256]{0:T(256)S(1)}, u32[256]{0:T(256)}, u32[]{:S(2)}) copy-start(u32[256]{0:T(256)} %constant.81) | copy-start | bytes 3076
  82.6 45.4 %copy-start.17 = (f32[32]{0:T(128)S(1)}, f32[32]{0:T(128)}, u32[]{:S(2)}) copy-start(f32[32]{0:T(128)} %param.29) | copy-start | bytes 388
  96.3 18.0 %all-to-all-start.3 = ((bf16[32,4,256]{2,1,0:T(4,128)(2,1)}), bf16[32,4,256]{2,1,0:T(4,128)(2,1)S(1)}, u32[]{:S(2)}, u32[]{:S(2)}) async-start(bf16[32,4,256]{2,1,0:T(4,128)(2,1)} %reshape.289), calls=%async_computation.3 | async-start | bytes 131072 | tf_op jit(solution)/shard_map/all_to_all | solution.py:146
  114.3 29.1 %all-to-all-start = ((bf16[64,8,256]{2,1,0:T(8,128)(2,1)}), bf16[64,8,256]{2,1,0:T(8,128)(2,1)S(1)}, u32[]{:S(2)}, u32[]{:S(2)}) async-start(bf16[64,8,256]{2,1,0:T(8,128)(2,1)} %param.17), calls=%async_computation | async-start | bytes 524288 | tf_op jit(solution)/shard_map/all_to_all | solution.py:75
  126.8 20.4 %copy-start.13 = (f32[256]{0:T(256)S(1)}, f32[256]{0:T(256)}, u32[]{:S(2)}) copy-start(f32[256]{0:T(256)} %param.19) | copy-start | bytes 3076
  138.6 9.6 %copy-start.16 = (bf16[256,2,32]{0,2,1:T(8,128)(2,1)S(1)}, bf16[256,2,32]{0,2,1:T(8,128)(2,1)}, u32[]{:S(2)}) copy-start(bf16[256,2,32]{0,2,1:T(8,128)(2,1)} %param.23) | copy-start | bytes 98308
  143.4 57.7 %all-to-all-start.4 = ((bf16[32,4,256]{2,0,1:T(8,128)(2,1)}), bf16[32,4,256]{2,0,1:T(8,128)(2,1)S(1)}, u32[]{:S(2)}, u32[]{:S(2)}) async-start(bf16[32,4,256]{2,0,1:T(8,128)(2,1)} %copy.63), calls=%async_computation.4 | async-start | bytes 131072 | tf_op jit(solution)/shard_map/all_to_all | solution.py:149
  146.7 81.5 %reduce-scatter.2.cloned.1.call-start = ((), (), s32[]{:S(2)}) async-start(), calls=%async_computation.7 | async-start | bytes 655360 | tf_op jit(solution)/shard_map/reduce_scatter | solution.py:143
  199.7 6.8 %copy-start.2 = (bf16[4,128,128]{2,1,0:T(8,128)(2,1)S(1)}, bf16[4,128,128]{2,1,0:T(8,128)(2,1)}, u32[]{:S(2)}) copy-start(bf16[4,128,128]{2,1,0:T(8,128)(2,1)} %get-tuple-element.12) | copy-start | bytes 393220
  199.7 6.8 %copy-start.3 = (bf16[4,128,128]{2,1,0:T(8,128)(2,1)S(1)}, bf16[4,128,128]{2,1,0:T(8,128)(2,1)}, u32[]{:S(2)}) copy-start(bf16[4,128,128]{2,1,0:T(8,128)(2,1)} %get-tuple-element.13) | copy-start | bytes 393220
  199.7 6.8 %copy-start.18 = (f32[128]{0:T(128)S(1)}, f32[128]{0:T(128)}, u32[]{:S(2)}) copy-start(f32[128]{0:T(128)} %param.31) | copy-start | bytes 1540
  200.3 22.5 %copy-start.7 = (bf16[256,256]{1,0:T(8,128)(2,1)S(1)}, bf16[256,256]{1,0:T(8,128)(2,1)}, u32[]{:S(2)}) copy-start(bf16[256,256]{1,0:T(8,128)(2,1)} %param.22) | copy-start | bytes 393220
  201.1 15.5 %all-to-all-start.1 = ((bf16[2,256,128]{2,0,1:T(2,128)(2,1)}), bf16[2,256,128]{2,0,1:T(2,128)(2,1)S(1)}, u32[]{:S(2)}, u32[]{:S(2)}) async-start(bf16[2,256,128]{2,0,1:T(2,128)(2,1)} %copy.56), calls=%async_computation.1 | async-start | bytes 262144 | tf_op jit(solution)/shard_map/all_to_all | solution.py:119
  216.6 11.6 %all-to-all-start.5 = ((bf16[8,32,128]{2,1,0:T(8,128)(2,1)}), bf16[8,32,128]{2,1,0:T(8,128)(2,1)S(1)}, u32[]{:S(2)}, u32[]{:S(2)}) async-start(bf16[8,32,128]{2,1,0:T(8,128)(2,1)} %bitcast.47), calls=%async_computation.5 | async-start | bytes 131072 | tf_op jit(solution)/shard_map/all_to_all | solution.py:166
  221.2 5.2 %collective-permute-start = (bf16[64,8,128]{2,1,0:T(8,128)(2,1)S(1)}, bf16[64,8,128]{2,1,0:T(8,128)(2,1)S(1)}, u32[]{:S(2)}, u32[]{:S(2)}) collective-permute-start(bf16[64,8,128]{2,1,0:T(8,128)(2,1)S(1)} %bitcast.216), channel_id=1, source_target_pairs={{0,128},{128,0},{1,129},{129,1},{2,130},{130,2},{3,131},{131,3},{4... | collective-permute-start | bytes 393224 | tf_op jit(solution)/shard_map/ppermute | solution.py:120
  (4 other events, 12.7 us)
Sparse Core Ops, SparseCore 0:
  198.6 18.5 reduce-scatter.1

commit v2 on v1

v2 whole, which is shorter than its diff:
```python
import jax
import jax.numpy as jnp
from jax import lax
from jax.sharding import PartitionSpec as P

EPSILON = 1e-05
BF = jnp.bfloat16
F32 = jnp.float32


def layer_normalize(values, axis):
    average = jnp.mean(values, axis=axis, keepdims=True)
    centred = values - average
    spread = jnp.mean(centred * centred, axis=axis, keepdims=True)
    return centred * lax.rsqrt(spread + EPSILON)


def exchange(values, axes):
    return lax.all_to_all(values, axes, split_axis=0, concat_axis=0, tiled=True)


def mm(a, b):
    return jnp.dot(a, b, preferred_element_type=F32)


def shards(
    alignment_input,
    pairwise_input,
    alignment_gain,
    product_gain,
    attention_weight,
    mixing_weight,
    outer_input_weight,
    outer_output_weight,
    bias_matrix,
    pairwise_gain,
    triangle_input_weight,
    triangle_gate_weight,
    triangle_gain,
    triangle_output_weight,
    transition_gain,
    transition_up_weight,
    transition_down_weight,
):
    sl, il, mw = alignment_input.shape
    cl, _, res = pairwise_input.shape
    pw, heads = bias_matrix.shape
    width = mixing_weight.shape[0]
    hd = width // heads
    pc = outer_input_weight.shape[2]
    rows = lax.axis_size("row")
    nq = lax.axis_size("seq")
    nb = lax.axis_size("branch")
    so = sl // rows
    hb = heads // nb
    wb = width // nb
    half = il // nb
    b = lax.axis_index("branch")
    q = lax.axis_index("seq")

    tl = transition_up_weight.shape[0]
    scaled_out = (triangle_output_weight.T.astype(F32) * triangle_gain[:, None]).astype(BF)
    packed = jnp.concatenate(
        [triangle_gate_weight, scaled_out, transition_up_weight, transition_down_weight.T], axis=0
    )
    wide = pairwise_input.reshape(cl * il, res)
    packed = jnp.concatenate(
        [wide[:, : res // 2], wide[:, res // 2 :], packed], axis=0
    )
    everyone = exchange(jnp.broadcast_to(packed[None], (nq,) + packed.shape), "seq")
    n = cl * il
    full = jnp.concatenate([everyone[:, :n], everyone[:, n : 2 * n]], axis=2).reshape(pw, il, res)
    packed = everyone[:, 2 * n :]
    gate_w = packed[:, :cl].reshape(pw, pw)
    out_wt = packed[:, cl : 2 * cl].reshape(pw, pw)
    up_w = packed[:, 2 * cl : 2 * cl + tl].reshape(nq * tl, pw)
    down_wt = packed[:, 2 * cl + tl :].reshape(nq * tl, pw)

    mine = lax.all_to_all(alignment_input, "row", split_axis=0, concat_axis=1, tiled=True)
    stat = layer_normalize(mine.astype(F32), 2)
    normed = (stat * alignment_gain).astype(BF).reshape(so * res, mw)
    outer_norm = (stat * product_gain).astype(BF)
    right = jnp.einsum(
        "sjm,md->dsj", outer_norm, outer_input_weight[:, 1], preferred_element_type=F32
    ).astype(BF)
    hr = res // nb
    right = lax.dynamic_slice_in_dim(right, hr * b, hr, 2).reshape(pc, so * hr)

    unit = layer_normalize(full.astype(F32), 0)
    plain = unit.astype(BF).reshape(pw, -1)
    tri_input = (unit * pairwise_gain[:, None, None]).astype(BF)
    bias_w = lax.dynamic_slice_in_dim(bias_matrix, hb * b, hb, 1)
    bias_own = lax.dot_general(
        bias_w, plain, (((0,), (0,)), ((), ())), preferred_element_type=F32
    ).astype(BF)
    tri_flat = tri_input.reshape(pw, -1)
    tri_half = lax.dynamic_slice_in_dim(tri_input, half * b, half, 1).reshape(pw, -1)
    lin_l = mm(triangle_input_weight[:2].reshape(2 * cl, pw), tri_half).reshape(2, cl, half, res)
    lin_r = mm(triangle_input_weight[2:].reshape(2 * cl, pw), tri_flat).reshape(2, cl, il, res)
    left_tri = (lin_l[0] * jax.nn.sigmoid(lin_l[1])).astype(BF)
    right_tri = (lin_r[0] * jax.nn.sigmoid(lin_r[1])).astype(BF)
    sent = jnp.concatenate(
        [
            jnp.broadcast_to(bias_own.reshape(1, hb * il, res), (rows, hb * il, res)),
            jnp.broadcast_to(right[None], (rows, pc, so * hr)),
            right_tri,
            left_tri,
        ],
        axis=1,
    )
    got = exchange(sent, "row")
    n = hb * il
    bias = got[:, :n].reshape(rows, hb, il, res).transpose(1, 0, 2, 3).reshape(hb, res, res)
    right = got[:, n : n + pc].reshape(rows, pc, so, hr).transpose(1, 0, 2, 3).reshape(pc, sl, hr)
    tri_r = got[:, n + pc : n + pc + il].reshape(rows * il, res)
    tri_l = got[:, n + pc + il :].reshape(rows * half, res)

    triangle = lax.dot_general(
        tri_l, tri_r, (((1,), (1,)), ((), ())), preferred_element_type=F32
    ).astype(BF)
    back = exchange(triangle.reshape(rows, half, res), "row")

    local = layer_normalize(alignment_input.astype(F32), 2)
    local = (local * product_gain).astype(BF).reshape(-1, mw)
    left = mm(local, outer_input_weight[:, 0]).astype(BF).reshape(sl, il * pc)
    prod = jnp.einsum("sk,dsj->kdj", left, right, preferred_element_type=F32).astype(BF)
    prod = prod.reshape(il, pc, pc, hr).transpose(0, 2, 1, 3).reshape(il, pc * pc, hr)
    w_outer = outer_output_weight.transpose(1, 0, 2).reshape(pc * pc, pw)
    outer = jnp.einsum("ikj,ko->oij", prod, w_outer, preferred_element_type=F32)
    outer = (outer * (1.0 / (sl * nq))).astype(BF).reshape(nq, cl * il, hr)

    back = back.transpose(1, 0, 2)
    send = jnp.concatenate([back[:, :, :hr], back[:, :, hr:], outer], axis=1)
    got = exchange(send, "seq")
    row_tri = jnp.concatenate([got[:, :cl], got[:, cl : 2 * cl]], axis=2).reshape(pw, res)
    outer_update = jnp.sum(got[:, 2 * cl :].astype(F32), axis=0).astype(BF).reshape(cl, il, hr)
    pick = half * b + q
    pair_row = lax.dynamic_slice_in_dim(full, pick, 1, 1).reshape(pw, res).astype(F32)
    tri_row = lax.dynamic_slice_in_dim(tri_input, pick, 1, 1).reshape(pw, res)
    tri_norm = layer_normalize(row_tri.astype(F32), 0).astype(BF)
    tri_out = lax.dot_general(
        out_wt, tri_norm, (((0,), (0,)), ((), ())), preferred_element_type=F32
    )
    first = (pair_row + jax.nn.sigmoid(mm(gate_w, tri_row)) * tri_out).astype(BF).astype(F32)
    trans = (layer_normalize(first, 0) * transition_gain[:, None]).astype(BF)
    hidden = jax.nn.relu(mm(up_w, trans)).astype(BF)
    pair_next = (
        first
        + lax.dot_general(down_wt, hidden, (((0,), (0,)), ((), ())), preferred_element_type=F32)
    ).astype(BF)
    parts = pair_next.reshape(nq, cl, nb, hr).transpose(2, 0, 1, 3).reshape(nb * nq, cl, hr)
    parts = exchange(parts, ("branch", "seq")).transpose(1, 0, 2)
    pairwise_output = (parts.astype(F32) + outer_update.astype(F32)).astype(BF)

    weights = lax.dynamic_slice_in_dim(attention_weight, wb * b, wb, 2)
    proj = mm(normed, weights.reshape(mw, 4 * wb)).reshape(so, res, 4, hb, hd)
    query = (proj[:, :, 0] * hd ** (-0.5)).astype(BF)
    keys = proj[:, :, 1].astype(BF)
    values = proj[:, :, 2].astype(BF)
    gate = jax.nn.sigmoid(proj[:, :, 3]).astype(BF)
    scores = jnp.einsum("sihd,sjhd->shij", query, keys, preferred_element_type=F32) + bias.astype(
        F32
    )
    top = jnp.max(scores, axis=3, keepdims=True)
    expo = jnp.exp(scores - top)
    totals = jnp.sum(expo, axis=3)
    weighted = jnp.einsum("shij,sjhd->sihd", expo.astype(BF), values, preferred_element_type=F32)
    mixed = (gate.astype(F32) * (weighted / totals.transpose(0, 2, 1)[..., None])).astype(BF)
    mixed = mixed.reshape(so, rows, il, wb).transpose(1, 0, 2, 3)
    mixed = jnp.broadcast_to(mixed[None], (nb,) + mixed.shape).reshape(nb * rows, so, il, wb)
    mixed = exchange(mixed, ("branch", "row")).reshape(nb, sl * il, wb)
    cols = lax.dynamic_slice_in_dim(mixing_weight, wb * b, wb, 1)
    residual = lax.dynamic_slice_in_dim(alignment_input, wb * b, wb, 2)
    projected = mm(mixed[0], cols[:wb]) + mm(mixed[1], cols[wb:])
    alignment_output = (residual.astype(F32) + projected.reshape(sl, il, wb)).astype(BF)
    return (alignment_output, pairwise_output)


def solution(mesh):
    return jax.shard_map(
        shards,
        mesh=mesh,
        in_specs=(
            P("seq", "row", None),
            P("seq", "row", None),
            P(),
            P(),
            P(),
            P(),
            P(),
            P(),
            P(),
            P(),
            P(None, "seq", None),
            P("seq", None),
            P("seq"),
            P(None, "seq"),
            P(),
            P("seq", None),
            P(None, "seq"),
        ),
        out_specs=(P("seq", "row", "branch"), P("seq", "row", "branch")),
        check_vma=False,
    )
```

time: 238 us -> 155 us (0.65)
  blocking collectives: 132 us -> 0 us
  waiting for transfers between devices: 12.3 us -> 65.7 us
  between operations: 15.4 us -> 1.3 us
  local copies, waits for them, and re-layouts: 14.9 us -> 22.7 us
  matrix products: 8.93 us -> 12.4 us
  starting transfers between devices: 46 us -> 43 us
    all_gather x5 -> x0, blocking collectives: 122 us -> none  [the longest x1 44.8 us: shards(): right = lax.all_gather(right, 'row', axis=0, tiled=True)]
    all_to_all x5 -> x6, waiting for transfers between devices: 8.89 us -> 59.3 us  [exchange(): return lax.all_to_all(values, axes, split_axis=0, concat_axis=0, tiled=True)]
    unnamed x1 -> x0, blocking collectives: 9.69 us -> none
    all_to_all x1, waiting for transfers between devices: 0.01 us -> 6.39 us  [shards(): lax.all_to_all(alignment_input, 'row', split_axis=0, concat_axis=1, tiled...]
    ppermute x1 -> x0, waiting for transfers between devices: 3.36 us -> none  [shards(): other = lax.ppermute(mixed, 'branch', [(i, i ^ 1) for i in range(nb)])]
    all_to_all x5 -> x6, starting transfers between devices: 32.7 us -> 30.1 us  [exchange(): return lax.all_to_all(values, axes, split_axis=0, concat_axis=0, tiled=True)]
    convert_element_type x1 -> x2, local copies, waits for them, and re-layouts: 0.2 us -> 2.72 us  [shards(): bias.astype(F32)]
    unnamed x49 -> x42, local copies, waits for them, and re-layouts: 4.75 us -> 7.05 us
  transfers between devices with their start and end apart: 8 -> 7, of which waited for: 2 -> 7; matrix products, arithmetic and copies ran while one was open for 10% -> 17% of each run, Pallas kernels for 0% -> 0%
where the time goes in v2:
time: 155 us; the launch traced here: 154 us
  waiting for transfers between devices  65.7 us (42%)
  starting transfers between devices  43 us (28%)
  local copies, waits for them, and re-layouts  22.7 us (15%)
  matrix products  12.4 us (8%)
  other arithmetic  8.65 us (6%)
    all_to_all x6, waiting for transfers between devices, exchange(): return lax.all_to_all(values, axes, split_axis=0, concat_axis=0, tiled=True)  59.3 us
    all_to_all x6, starting transfers between devices, exchange(): return lax.all_to_all(values, axes, split_axis=0, concat_axis=0, tiled=True)  30.1 us
    all_to_all x1, starting transfers between devices, shards(): lax.all_to_all(alignment_input, 'row', split_axis=0, concat_axis=1, tiled...  12.9 us
    unnamed x42, local copies, waits for them, and re-layouts  7.05 us
    all_to_all x1, waiting for transfers between devices, shards(): lax.all_to_all(alignment_input, 'row', split_axis=0, concat_axis=1, tiled...  6.39 us
    dot_general x7, matrix products, mm(): return jnp.dot(a, b, preferred_element_type=F32)  5.44 us
  transfers between devices with their start and end apart: 7, of which 7 were waited for; matrix products, arithmetic and copies ran while one was open for 17% of the time, Pallas kernels for 0%

profile of v2, /device:TPU:1, one launch (start us, length us, event | category | flops | bytes accessed | tf_op | source)
XLA Modules:
  0.0 153.7 jit_solution(2095982086315962033)
XLA Ops:
  0.6 12.9 %all-to-all-start = ((bf16[64,8,256]{2,1,0:T(8,128)(2,1)}), bf16[64,8,256]{2,1,0:T(8,128)(2,1)S(1)}, u32[]{:S(2)}, u32[]{:S(2)}) async-start(bf16[64,8,256]{2,1,0:T(8,128)(2,1)} %param.17), calls=%async_computation | async-start | bytes 524288 | tf_op jit(solution)/shard_map/all_to_all | solution.py:79
  20.1 6.4 %all-to-all-done = bf16[64,8,256]{2,1,0:T(8,128)(2,1)S(1)} async-done(((bf16[64,8,256]{2,1,0:T(8,128)(2,1)}), bf16[64,8,256]{2,1,0:T(8,128)(2,1)S(1)}, u32[]{:S(2)}, u32[]{:S(2)}) %all-to-all-start) | async-done | bytes 262176 | tf_op jit(solution)/shard_map/all_to_all | solution.py:79
  27.5 4.0 %all-to-all-start.1 = ((bf16[4,832,128]{2,1,0:T(8,128)(2,1)}), bf16[4,832,128]{2,1,0:T(8,128)(2,1)S(1)}, u32[]{:S(2)}, u32[]{:S(2)}) async-start(bf16[4,832,128]{2,1,0:T(8,128)(2,1)} %broadcast_in_dim.12), calls=%async_computation.1 | async-start | bytes 1703936 | tf_op jit(solution)/shard_map/all_to_all | solution.py:19
  33.2 10.8 %all-to-all-done.1 = bf16[4,832,128]{2,1,0:T(8,128)(2,1)S(1)} async-done(((bf16[4,832,128]{2,1,0:T(8,128)(2,1)}), bf16[4,832,128]{2,1,0:T(8,128)(2,1)S(1)}, u32[]{:S(2)}, u32[]{:S(2)}) %all-to-all-start.1) | async-done | bytes 852000 | tf_op jit(solution)/shard_map/all_to_all | solution.py:19
  49.2 1.2 pad_maximum_fusion
  50.4 5.1 %all-to-all-start.2 = ((bf16[32,76,256]{2,1,0:T(8,128)(2,1)}), bf16[32,76,256]{2,1,0:T(8,128)(2,1)S(1)}, u32[]{:S(2)}, u32[]{:S(2)}) async-start(bf16[32,76,256]{2,1,0:T(8,128)(2,1)} %pad_maximum_fusion), calls=%async_computation.2 | async-start | bytes 2621440 | tf_op jit(solution)/shard_map/all_to_all | solution.py:19
  57.5 2.5 %fusion.118 = (bf16[2,256,4,4,32]{1,4,3,2,0:T(8,128)(2,1)}, f32[2,256,4,4,32]{1,4,3,2,0:T(8,128)}) fusion(bf16[4,4,32,256,1]{3,2,1,0,4:T(8,128)(2,1)} %bitcast.204, bf16[2,32,8,256]{3,2,0,1:T(8,128)(2,1)} %get-tuple-element.15), kind=kOutput, calls=%fused_computation.180 | convolution fusion | flops 134479872 | bytes 2097152 | tf_op jit(solution)/shard_map/dot_general | solution.py:23
  60.0 2.0 %constant_dynamic-slice_fusion = (bf16[128,1,256]{2,1,0:T(2,128)(2,1)}, bf16[128,1,256]{2,1,0:T(2,128)(2,1)}) fusion(bf16[128,8,256]{2,1,0:T(8,128)(2,1)} %fusion.26, s32[]{:T(128)S(6)} %select_n.16, bf16[128,8,256]{2,1,0:T(8,128)(2,1)S(1)} %bitcast.195), kind=kLoop, calls=%fused_computation.158 | loop fusion | bytes 262148 | tf_op jit(solution)/shard_map/dynamic_slice | solution.py:139
  62.8 26.2 %all-to-all-done.2 = bf16[32,76,256]{2,1,0:T(8,128)(2,1)S(1)} async-done(((bf16[32,76,256]{2,1,0:T(8,128)(2,1)}), bf16[32,76,256]{2,1,0:T(8,128)(2,1)S(1)}, u32[]{:S(2)}, u32[]{:S(2)}) %all-to-all-start.2) | async-done | bytes 1245216 | tf_op jit(solution)/shard_map/all_to_all | solution.py:19
  89.9 6.1 %all-to-all-start.4 = ((bf16[32,4,256]{2,1,0:T(4,128)(2,1)}), bf16[32,4,256]{2,1,0:T(4,128)(2,1)}, u32[]{:S(2)}, u32[]{:S(2)}) async-start(bf16[32,4,256]{2,1,0:T(4,128)(2,1)} %reshape.340), calls=%async_computation.4 | async-start | bytes 131072 | tf_op jit(solution)/shard_map/all_to_all | solution.py:19
  98.4 1.1 copy.142
  99.5 1.6 %copy.93 = f32[4,256,256]{1,2,0:T(8,128)S(1)} copy(f32[4,256,256]{2,1,0:T(8,128)} %bitcast.196) | data formatting | bytes 2097152 | tf_op jit(solution)/shard_map/convert_element_type | solution.py:161
  101.1 4.8 %all-to-all-done.4 = bf16[32,4,256]{2,1,0:T(4,128)(2,1)} async-done(((bf16[32,4,256]{2,1,0:T(4,128)(2,1)}), bf16[32,4,256]{2,1,0:T(4,128)(2,1)}, u32[]{:S(2)}, u32[]{:S(2)}) %all-to-all-start.4) | async-done | bytes 65568 | tf_op jit(solution)/shard_map/all_to_all | solution.py:19
  107.5 4.1 %all-to-all-start.5 = ((bf16[4,320,128]{2,1,0:T(8,128)(2,1)}), bf16[4,320,128]{2,1,0:T(8,128)(2,1)}, u32[]{:S(2)}, u32[]{:S(2)}) async-start(bf16[4,320,128]{2,1,0:T(8,128)(2,1)} %pad_maximum_fusion.2), calls=%async_computation.5 | async-start | bytes 655360 | tf_op jit(solution)/shard_map/all_to_all | solution.py:19
  111.7 1.4 add_reduce_fusion
  113.1 1.3 copy-done.1
  114.8 4.0 %all-to-all-done.5 = bf16[4,320,128]{2,1,0:T(8,128)(2,1)} async-done(((bf16[4,320,128]{2,1,0:T(8,128)(2,1)}), bf16[4,320,128]{2,1,0:T(8,128)(2,1)}, u32[]{:S(2)}, u32[]{:S(2)}) %all-to-all-start.5) | async-done | bytes 327712 | tf_op jit(solution)/shard_map/all_to_all | solution.py:19
  119.9 1.2 fusion.119
  121.1 1.4 fusion.22
  123.2 3.4 %all-to-all-start.6 = ((bf16[8,32,128]{2,1,0:T(8,128)(2,1)}), bf16[8,32,128]{2,1,0:T(8,128)(2,1)S(1)}, u32[]{:S(2)}, u32[]{:S(2)}) async-start(bf16[8,32,128]{2,1,0:T(8,128)(2,1)} %bitcast.58), calls=%async_computation.6 | async-start | bytes 131072 | tf_op jit(solution)/shard_map/all_to_all | solution.py:19
  126.6 2.1 %fusion.14 = bf16[2,256,4,32]{1,3,2,0:T(8,128)(2,1)S(1)} fusion(f32[2,4,256,256]{2,3,1,0:T(8,128)} %copy-done.1, f32[2,4,256]{2,1,0:T(4,128)S(1)} %get-tuple-element.28, f32[4,256,256]{1,2,0:T(8,128)S(1)} %copy.93, bf16[2,256,4,4,32]{1,4,3,2,0:T(8,128)(2,1)} %get-tuple-element.26, f32[2,256,4]{1,2,0:T(4,128)S(1)} %bitcast.221, ...), kind=kOutput, calls=%fused_computation.27 | convolution fusion | flops 35651584 | bytes 3686400 | tf_op jit(solution)/shard_map/shij,sjhd->sihd/dot_general | solution.py:167
  129.4 2.4 %all-to-all-done.6 = bf16[8,32,128]{2,1,0:T(8,128)(2,1)S(1)} async-done(((bf16[8,32,128]{2,1,0:T(8,128)(2,1)}), bf16[8,32,128]{2,1,0:T(8,128)(2,1)S(1)}, u32[]{:S(2)}, u32[]{:S(2)}) %all-to-all-start.6) | async-done | bytes 65568 | tf_op jit(solution)/shard_map/all_to_all | solution.py:19
  132.5 7.4 %all-to-all-start.3 = ((bf16[64,2,8,128]{3,2,1,0:T(8,128)(2,1)}), bf16[64,2,8,128]{3,2,1,0:T(8,128)(2,1)S(1)}, u32[]{:S(2)}, u32[]{:S(2)}) async-start(bf16[64,2,8,128]{3,2,1,0:T(8,128)(2,1)} %bitcast.35), calls=%async_computation.3 | async-start | bytes 524288 | tf_op jit(solution)/shard_map/all_to_all | solution.py:19
  141.5 11.2 %all-to-all-done.3 = bf16[64,2,8,128]{3,2,1,0:T(8,128)(2,1)S(1)} async-done(((bf16[64,2,8,128]{3,2,1,0:T(8,128)(2,1)}), bf16[64,2,8,128]{3,2,1,0:T(8,128)(2,1)S(1)}, u32[]{:S(2)}, u32[]{:S(2)}) %all-to-all-start.3) | async-done | bytes 262176 | tf_op jit(solution)/shard_map/all_to_all | solution.py:19
  (123 shorter events, 27.9 us)
Async XLA Ops:
  0.6 55.9 %copy-start = (bf16[256,4,256]{2,1,0:T(4,128)(2,1)S(1)}, bf16[256,4,256]{2,1,0:T(4,128)(2,1)}, u32[]{:S(2)}) copy-start(bf16[256,4,256]{2,1,0:T(4,128)(2,1)} %param.21) | copy-start | bytes 1572868
  0.6 25.8 %all-to-all-start = ((bf16[64,8,256]{2,1,0:T(8,128)(2,1)}), bf16[64,8,256]{2,1,0:T(8,128)(2,1)S(1)}, u32[]{:S(2)}, u32[]{:S(2)}) async-start(bf16[64,8,256]{2,1,0:T(8,128)(2,1)} %param.17), calls=%async_computation | async-start | bytes 524288 | tf_op jit(solution)/shard_map/all_to_all | solution.py:79
  13.5 18.5 %copy-start.11 = (f32[256]{0:T(256)S(1)}, f32[256]{0:T(256)}, u32[]{:S(2)}) copy-start(f32[256]{0:T(256)} %param.19) | copy-start | bytes 3076
  13.6 18.5 %copy-start.12 = (f32[256]{0:T(256)S(1)}, f32[256]{0:T(256)}, u32[]{:S(2)}) copy-start(f32[256]{0:T(256)} %param.20) | copy-start | bytes 3076
  20.1 12.9 %copy-start.15 = (bf16[256,2,32]{0,2,1:T(8,128)(2,1)S(1)}, bf16[256,2,32]{0,2,1:T(8,128)(2,1)}, u32[]{:S(2)}) copy-start(bf16[256,2,32]{0,2,1:T(8,128)(2,1)} %param.23) | copy-start | bytes 98308
  27.5 16.4 %all-to-all-start.1 = ((bf16[4,832,128]{2,1,0:T(8,128)(2,1)}), bf16[4,832,128]{2,1,0:T(8,128)(2,1)S(1)}, u32[]{:S(2)}, u32[]{:S(2)}) async-start(bf16[4,832,128]{2,1,0:T(8,128)(2,1)} %broadcast_in_dim.12), calls=%async_computation.1 | async-start | bytes 1703936 | tf_op jit(solution)/shard_map/all_to_all | solution.py:19
  43.9 0.9 copy-start.2
  44.0 1.4 copy-start.10
  46.9 1.0 copy-start.8
  49.2 6.4 %copy-start.5 = (bf16[64,8,256]{2,1,0:T(8,128)(2,1)S(1)}, bf16[64,8,256]{2,1,0:T(8,128)(2,1)}, u32[]{:S(2)}) copy-start(bf16[64,8,256]{2,1,0:T(8,128)(2,1)} %param.17) | copy-start | bytes 786436
  50.4 38.7 %all-to-all-start.2 = ((bf16[32,76,256]{2,1,0:T(8,128)(2,1)}), bf16[32,76,256]{2,1,0:T(8,128)(2,1)S(1)}, u32[]{:S(2)}, u32[]{:S(2)}) async-start(bf16[32,76,256]{2,1,0:T(8,128)(2,1)} %pad_maximum_fusion), calls=%async_computation.2 | async-start | bytes 2621440 | tf_op jit(solution)/shard_map/all_to_all | solution.py:19
  56.3 5.8 %copy-start.3 = (bf16[4,832,128]{2,1,0:T(8,128)(2,1)S(1)}, bf16[4,832,128]{2,1,0:T(8,128)(2,1)}, u32[]{:S(2)}) copy-start(bf16[4,832,128]{2,1,0:T(8,128)(2,1)} %copy-done.2) | copy-start | bytes 2555908
  89.9 16.0 %all-to-all-start.4 = ((bf16[32,4,256]{2,1,0:T(4,128)(2,1)}), bf16[32,4,256]{2,1,0:T(4,128)(2,1)}, u32[]{:S(2)}, u32[]{:S(2)}) async-start(bf16[32,4,256]{2,1,0:T(4,128)(2,1)} %reshape.340), calls=%async_computation.4 | async-start | bytes 131072 | tf_op jit(solution)/shard_map/all_to_all | solution.py:19
  96.4 1.3 copy-start.14
  99.5 12.2 %copy-start.7 = (f32[2,256,4,4,32]{1,4,3,2,0:T(8,128)S(1)}, f32[2,256,4,4,32]{1,4,3,2,0:T(8,128)}, u32[]{:S(2)}) copy-start(f32[2,256,4,4,32]{1,4,3,2,0:T(8,128)} %get-tuple-element.27) | copy-start | bytes 3145732
  107.5 11.2 %all-to-all-start.5 = ((bf16[4,320,128]{2,1,0:T(8,128)(2,1)}), bf16[4,320,128]{2,1,0:T(8,128)(2,1)}, u32[]{:S(2)}, u32[]{:S(2)}) async-start(bf16[4,320,128]{2,1,0:T(8,128)(2,1)} %pad_maximum_fusion.2), calls=%async_computation.5 | async-start | bytes 655360 | tf_op jit(solution)/shard_map/all_to_all | solution.py:19
  113.1 1.3 copy-start.1
  113.1 6.6 %copy-start.4 = (bf16[4,832,128]{2,1,0:T(8,128)(2,1)S(1)}, bf16[4,832,128]{2,1,0:T(8,128)(2,1)}, u32[]{:S(2)}) copy-start(bf16[4,832,128]{2,1,0:T(8,128)(2,1)} %copy-done.2) | copy-start | bytes 2555908
  113.1 6.8 %slice-start = ((bf16[4,832,128]{2,1,0:T(8,128)(2,1)}), bf16[4,32,128]{2,1,0:T(8,128)(2,1)S(1)}, s32[]{:S(2)}) async-start(bf16[4,832,128]{2,1,0:T(8,128)(2,1)} %copy-done.2), calls=%async_computation.7 | async-start | bytes 65536 | tf_op jit(solution)/shard_map/slice | solution.py:74
  114.4 6.7 %copy-start.16 = (f32[128]{0:T(128)S(1)}, f32[128]{0:T(128)}, u32[]{:S(2)}) copy-start(f32[128]{0:T(128)} %param.31) | copy-start | bytes 1540
  123.2 8.5 %all-to-all-start.6 = ((bf16[8,32,128]{2,1,0:T(8,128)(2,1)}), bf16[8,32,128]{2,1,0:T(8,128)(2,1)S(1)}, u32[]{:S(2)}, u32[]{:S(2)}) async-start(bf16[8,32,128]{2,1,0:T(8,128)(2,1)} %bitcast.58), calls=%async_computation.6 | async-start | bytes 131072 | tf_op jit(solution)/shard_map/all_to_all | solution.py:19
  128.7 24.0 %copy-start.9 = (bf16[256,256]{1,0:T(8,128)(2,1)S(1)}, bf16[256,256]{1,0:T(8,128)(2,1)}, u32[]{:S(2)}) copy-start(bf16[256,256]{1,0:T(8,128)(2,1)} %param.22) | copy-start | bytes 393220
  128.7 24.2 %copy-start.6 = (bf16[64,8,256]{2,1,0:T(8,128)(2,1)S(1)}, bf16[64,8,256]{2,1,0:T(8,128)(2,1)}, u32[]{:S(2)}) copy-start(bf16[64,8,256]{2,1,0:T(8,128)(2,1)} %param.17) | copy-start | bytes 786436
  132.5 20.2 %all-to-all-start.3 = ((bf16[64,2,8,128]{3,2,1,0:T(8,128)(2,1)}), bf16[64,2,8,128]{3,2,1,0:T(8,128)(2,1)S(1)}, u32[]{:S(2)}, u32[]{:S(2)}) async-start(bf16[64,2,8,128]{3,2,1,0:T(8,128)(2,1)} %bitcast.35), calls=%async_computation.3 | async-start | bytes 524288 | tf_op jit(solution)/shard_map/all_to_all | solution.py:19
  (1 other events, 0.9 us)

commit v3 on v1

v3 whole, which is shorter than its diff:
```python
import jax
import jax.numpy as jnp
from jax import lax
from jax.experimental import pallas as pl
from jax.experimental.pallas import tpu as pltpu
from jax.sharding import PartitionSpec as P

EPSILON = 1e-05
BF = jnp.bfloat16
F32 = jnp.float32
NZ, NW = 8, 4
NR = NZ * NW
NQ = 4


def mm(a, b):
    return jnp.dot(a, b, preferred_element_type=F32)


def mm_t(a, b):
    return lax.dot_general(a, b, (((1,), (1,)), ((), ())), preferred_element_type=F32)


def normalize(x, axis):
    average = jnp.mean(x, axis=axis, keepdims=True)
    centred = x - average
    spread = jnp.mean(centred * centred, axis=axis, keepdims=True)
    return centred * lax.rsqrt(spread + EPSILON)


def body(
    a_ref,
    p_ref,
    ag_ref,
    pg_ref,
    aw_ref,
    mw_ref,
    ol_ref,
    or_ref,
    oo_ref,
    bm_ref,
    col_ref,
    ti_ref,
    tg_ref,
    tn_ref,
    to_ref,
    up_ref,
    dn_ref,
    msa_ref,
    pair_ref,
    g,
    w,
    tin,
    lt,
    rt,
    ls,
    rs,
    bs,
    lb,
    rb,
    bf,
    mn,
    lx,
    lxt,
    qkv,
    rg,
    rgt,
    pq,
    ob,
    orb,
    tb,
    bk,
    xs,
    xr,
    pn,
    fb,
    mx,
    ao,
    mo,
    ss,
    rv,
):
    b = lax.axis_index("branch")
    r = lax.axis_index("row")
    q = lax.axis_index("seq")
    zi = r // NW
    wi = r % NW
    inside = (r // (NR // 2)) == b
    cols = pl.ds(pl.multiple_of(b * 128, 128), 128)

    def signal(where):
        pl.semaphore_signal(
            barrier, inc=1, device_id=where, device_id_type=pl.DeviceIdType.MESH
        )

    def send(src, dst, k, where):
        pltpu.make_async_remote_copy(
            src_ref=src,
            dst_ref=dst,
            send_sem=ss.at[k],
            recv_sem=rv.at[k],
            device_id=where,
            device_id_type=pl.DeviceIdType.MESH,
        ).start()

    def arrived(view, k):
        pltpu.make_async_copy(view, view, rv.at[k]).wait()

    def left_here(view, k):
        pltpu.make_async_copy(view, view, ss.at[k]).wait()

    def row_peers(do):
        def step(k, carry):
            do(lax.rem(r + k, NR))
            return carry

        lax.fori_loop(1, NR, step, 0)

    barrier = pltpu.get_barrier_semaphore()
    row_peers(lambda peer: signal({"row": peer}))
    for k in range(1, NQ):
        signal({"seq": lax.rem(q + k, NQ)})
    signal({"branch": 1 - b})

    g[q] = jnp.transpose(p_ref[...].astype(F32), (1, 0, 2)).astype(BF)
    w[q, 0:32] = tg_ref[...]
    w[q, 32:160] = jnp.zeros((128, 128), BF)
    w[q, 32:160, 0:32] = (to_ref[...].astype(F32) * tn_ref[...]).astype(BF)
    w[q, 160:288] = up_ref[...]
    w[q, 288:416] = dn_ref[...]
    for s in range(2):
        mn[r, s] = a_ref[s, r]

    pl.semaphore_wait(barrier, NR - 1 + NQ - 1 + 1)

    for k in range(1, NQ):
        send(g.at[q], g.at[q], 0, {"seq": lax.rem(q + k, NQ)})
    row_peers(lambda peer: send(a_ref.at[:, peer], mn.at[r], 1, {"row": peer}))
    for k in range(1, NQ):
        send(w.at[q], w.at[q], 2, {"seq": lax.rem(q + k, NQ)})

    lane = lax.broadcasted_iota(jnp.int32, (16, 8, 256), 2) // 32
    sub = lax.broadcasted_iota(jnp.int32, (16, 8, 256), 1)
    for s in range(2):
        for k in range(2):
            x = a_ref[s, 16 * k : 16 * k + 16].astype(F32).reshape(128, 256)
            x = (normalize(x, 1) * pg_ref[...]).astype(BF)
            x = mm(x, ol_ref[...]).reshape(16, 8, 256)
            lx[32 * s + 16 * k : 32 * s + 16 * k + 16] = jnp.sum(
                jnp.where(lane == sub, x, 0.0), axis=1
            )
    lxt[...] = jnp.transpose(lx[...]).astype(BF)

    arrived(g.at[pl.ds(0, NQ - 1)], 0)
    head = NQ * b + q
    head_row = lax.broadcasted_iota(jnp.int32, (8, 128), 0)
    column = jnp.sum(jnp.where(head_row == head, bm_ref[...], 0.0), axis=0, keepdims=True)

    def pair_row(i, acc):
        unit = normalize(g[:, i].astype(F32).reshape(128, 256), 0)
        pick = jnp.where(head_row == i, column, 0.0).astype(BF)
        acc = acc + mm(pick, unit.astype(BF))
        tri = (unit * col_ref[:, 0:1]).astype(BF)
        tin[i] = tri
        lin = mm(ti_ref[...].reshape(128, 128), tri)
        lt[i] = lin[0:32] * jax.nn.sigmoid(lin[32:64])
        rt[i] = lin[64:96] * jax.nn.sigmoid(lin[96:128])
        return acc

    bs[...] = lax.fori_loop(0, 8, pair_row, jnp.zeros((8, 256), F32)).astype(BF)
    ls[...] = jnp.transpose(lt[...], (1, 0, 2)).astype(BF)
    rs[...] = jnp.transpose(rt[...], (1, 0, 2)).astype(BF)
    lb[r] = ls[r]
    bf[q, r] = bs[...]

    row_peers(lambda peer: send(ls.at[peer], lb.at[r], 3, {"row": peer}))

    @pl.when(inside)
    def _():
        rb[r % (NR // 2)] = rs[r]
        row_peers(lambda peer: send(rs.at[peer], rb.at[r % (NR // 2)], 4, {"row": peer}))

    row_peers(lambda peer: send(bs, bf.at[q, r], 5, {"row": peer}))

    arrived(mn.at[pl.ds(0, NR - 1)], 1)
    for s in range(2):
        x = normalize(mn[:, s].astype(F32).reshape(256, 256), 1)
        normed = (x * ag_ref[...]).astype(BF)
        qkv[s, 0] = (mm(normed, aw_ref[0]) * (32.0**-0.5)).astype(BF)
        qkv[s, 1] = mm(normed, aw_ref[1]).astype(BF)
        qkv[s, 2] = mm(normed, aw_ref[2]).astype(BF)
        qkv[s, 3] = jax.nn.sigmoid(mm(normed, aw_ref[3])).astype(BF)
        right = mm_t(or_ref[...], (x * pg_ref[...]).astype(BF))
        rg[zi, wi, s] = jnp.where(b == 0, right[:, :128], right[:, 128:]).astype(BF)

    def z_peers(k, carry):
        send(rg.at[zi, wi], rg.at[zi, wi], 8, {"row": lax.rem(zi + k, NZ) * NW + wi})
        return carry

    lax.fori_loop(1, NZ, z_peers, 0)

    arrived(lb.at[pl.ds(0, NR - 1)], 3)

    @pl.when(inside)
    def _():
        arrived(rb.at[pl.ds(0, NR // 2 - 1)], 4)

    @pl.when(jnp.logical_not(inside))
    def _():
        arrived(rb, 4)

    tl = lb[...].astype(F32).reshape(256, 256).astype(BF)
    tr = rb[...].astype(F32).reshape(128, 256).astype(BF)
    tb[...] = mm_t(tl, tr).reshape(32, 8, 128).astype(BF)
    bk[r] = tb[r]
    row_peers(lambda peer: send(tb.at[peer], bk.at[r], 6, {"row": peer}))

    arrived(bf.at[0, pl.ds(0, NR - 1)], 5)
    for k in range(1, NQ):
        send(bf.at[q], bf.at[q], 7, {"seq": lax.rem(q + k, NQ)})

    arrived(rg.at[pl.ds(0, NZ - 1), 0], 8)
    for k in range(1, NW):
        send(rg.at[:, wi], rg.at[:, wi], 9, {"row": zi * NW + lax.rem(wi + k, NW)})

    arrived(bk.at[pl.ds(0, NR - 1)], 6)
    xs[...] = jnp.transpose(bk[...].astype(F32), (1, 0, 2)).astype(BF)
    xr[q] = xs[pl.ds(2 * q, 2)]
    for k in range(1, NQ):
        peer = lax.rem(q + k, NQ)
        send(xs.at[pl.ds(2 * peer, 2)], xr.at[q], 10, {"seq": peer})

    arrived(rg.at[:, pl.ds(0, NW - 1)], 9)
    for s in range(2):
        x = rg[:, :, s].astype(F32).reshape(32, 32, 128)
        rgt[:, 32 * s : 32 * s + 32] = jnp.transpose(x, (1, 0, 2)).astype(BF)

    def outer_step(d, carry):
        x = mm(lxt[...], rgt[d]).astype(BF)
        pq[:, pl.ds(pl.multiple_of(d * 32, 32), 32)] = x.reshape(8, 32, 128)
        return carry

    lax.fori_loop(0, 32, outer_step, 0)

    arrived(xr.at[pl.ds(0, NQ - 1)], 10)
    arrived(w.at[pl.ds(0, NQ - 1)], 2)
    row_tri = jnp.concatenate(
        [xr[:, i].astype(F32).reshape(128, 128) for i in range(2)], axis=1
    )
    pair_in = jnp.concatenate(
        [g[:, 2 * q + i, :, cols].astype(F32).reshape(128, 128) for i in range(2)], axis=1
    )
    tri_row = jnp.concatenate([tin[2 * q + i, :, cols] for i in range(2)], axis=1)
    tri_norm = normalize(row_tri, 0).astype(BF)
    tri_out = mm(w[0, 32:160, 0:32], tri_norm[0:32])
    for k in range(1, NQ):
        tri_out = tri_out + mm(w[k, 32:160, 0:32], tri_norm[32 * k : 32 * k + 32])
    gate = jax.nn.sigmoid(mm(w[:, 0:32].reshape(128, 128), tri_row))
    first = (pair_in + gate * tri_out).astype(BF).astype(F32)
    trans = (normalize(first, 0) * col_ref[:, 1:2]).astype(BF)
    moved = first
    for k in range(NQ):
        hidden = jnp.maximum(mm(w[k, 160:288], trans), 0.0).astype(BF)
        moved = moved + mm(w[k, 288:416], hidden)
    moved = moved.astype(BF)
    for i in range(2):
        pn[:, i] = moved[:, 128 * i : 128 * i + 128].reshape(4, 32, 128)
    fb[pl.ds(2 * q, 2)] = pn[q]
    for k in range(1, NQ):
        peer = lax.rem(q + k, NQ)
        send(pn.at[peer], fb.at[pl.ds(2 * q, 2)], 11, {"seq": peer})

    arrived(bf.at[pl.ds(0, NQ - 1)], 7)
    lane_head = lax.broadcasted_iota(jnp.int32, (256, 128), 1) // 32
    for s in range(2):

        def one_head(h, acc):
            here = lane_head == h
            query = jnp.where(here, qkv[s, 0].astype(F32), 0.0).astype(BF)
            score = mm_t(query, qkv[s, 1]) + bf[h].astype(F32).reshape(256, 256)
            expo = jnp.exp(score - jnp.max(score, axis=1, keepdims=True))
            total = jnp.sum(expo, axis=1, keepdims=True)
            value = mm(expo.astype(BF), qkv[s, 2]) / total
            return jnp.where(here, value, acc)

        value = lax.fori_loop(0, 4, one_head, jnp.zeros((256, 128), F32))
        mx[b, s] = (qkv[s, 3].astype(F32) * value).astype(BF)
    send(mx.at[b], mx.at[b], 13, {"branch": 1 - b})

    def project_step(i, carry):
        x = mm(oo_ref[...], pq[i]) * (1.0 / 256.0)
        ob[:, i] = x.astype(BF).reshape(4, 32, 128)
        return carry

    lax.fori_loop(0, 8, project_step, 0)
    orb[q] = ob[q]
    for k in range(1, NQ):
        peer = lax.rem(q + k, NQ)
        send(ob.at[peer], orb.at[q], 12, {"seq": peer})

    arrived(mx.at[0], 13)
    for s in range(2):
        x = mm(mx[0, s], mw_ref[0:128, cols]) + mm(mx[1, s], mw_ref[128:256, cols])
        x = mn[:, s, :, cols].astype(F32).reshape(256, 128) + x
        ao[:, s] = x.reshape(32, 8, 128).astype(BF)
        mo[s, r] = ao[r, s]
    row_peers(lambda peer: send(ao.at[peer], mo.at[:, r], 14, {"row": peer}))

    arrived(fb.at[pl.ds(0, 6)], 11)
    arrived(orb.at[pl.ds(0, NQ - 1)], 12)
    update = orb[0].astype(F32)
    for k in range(1, NQ):
        update = update + orb[k].astype(F32)
    update = update.astype(BF).astype(F32) + fb[...].astype(F32)
    pair_ref[...] = jnp.transpose(update, (1, 0, 2)).astype(BF)

    arrived(mo.at[:, pl.ds(0, NR - 1)], 14)
    msa_ref[...] = mo[...]

    for k, view in (
        (0, g.at[pl.ds(0, NQ - 1)]),
        (1, mn.at[pl.ds(0, NR - 1)]),
        (2, w.at[pl.ds(0, NQ - 1)]),
        (3, lb.at[pl.ds(0, NR - 1)]),
        (5, bf.at[0, pl.ds(0, NR - 1)]),
        (6, bk.at[pl.ds(0, NR - 1)]),
        (7, bf.at[pl.ds(0, NQ - 1)]),
        (8, rg.at[pl.ds(0, NZ - 1), 0]),
        (9, rg.at[:, pl.ds(0, NW - 1)]),
        (10, xr.at[pl.ds(0, NQ - 1)]),
        (11, fb.at[pl.ds(0, 6)]),
        (12, orb.at[pl.ds(0, NQ - 1)]),
        (13, mx.at[0]),
        (14, mo.at[:, pl.ds(0, NR - 1)]),
    ):
        left_here(view, k)

    @pl.when(inside)
    def _():
        left_here(lb.at[pl.ds(0, NR - 1)], 4)


def shards(
    alignment_input,
    pairwise_input,
    alignment_gain,
    product_gain,
    attention_weight,
    mixing_weight,
    outer_input_weight,
    outer_output_weight,
    bias_matrix,
    pairwise_gain,
    triangle_input_weight,
    triangle_gate_weight,
    triangle_gain,
    triangle_output_weight,
    transition_gain,
    transition_up_weight,
    transition_down_weight,
):
    b = lax.axis_index("branch")
    operands = (
        alignment_input.reshape(2, NR, 8, 256),
        pairwise_input,
        alignment_gain.reshape(1, 256),
        product_gain.reshape(1, 256),
        lax.dynamic_slice_in_dim(attention_weight, 128 * b, 128, 2).transpose(1, 0, 2),
        mixing_weight,
        jnp.tile(outer_input_weight[:, 0], (1, 8)),
        outer_input_weight[:, 1].T,
        outer_output_weight.transpose(2, 1, 0).reshape(128, 1024),
        bias_matrix.T.astype(F32),
        jnp.stack([pairwise_gain, transition_gain], axis=1),
        triangle_input_weight,
        triangle_gate_weight,
        triangle_gain.reshape(1, 32),
        triangle_output_weight,
        transition_up_weight,
        transition_down_weight,
    )
    vm = pltpu.VMEM
    msa, pair = pl.pallas_call(
        body,
        out_shape=(
            jax.ShapeDtypeStruct((2, NR, 8, 128), BF),
            jax.ShapeDtypeStruct((32, 8, 128), BF),
        ),
        in_specs=[pl.BlockSpec(memory_space=pltpu.VMEM)] * len(operands),
        out_specs=[pl.BlockSpec(memory_space=pltpu.VMEM)] * 2,
        scratch_shapes=[
            vm((4, 8, 32, 256), BF),
            vm((4, 416, 128), BF),
            vm((8, 128, 256), BF),
            vm((8, 32, 256), F32),
            vm((8, 32, 256), F32),
            vm((32, 8, 256), BF),
            vm((32, 8, 256), BF),
            vm((8, 256), BF),
            vm((32, 8, 256), BF),
            vm((16, 8, 256), BF),
            vm((4, 32, 8, 256), BF),
            vm((32, 2, 8, 256), BF),
            vm((64, 256), F32),
            vm((256, 64), BF),
            vm((2, 4, 256, 128), BF),
            vm((8, 4, 2, 32, 128), BF),
            vm((32, 64, 128), BF),
            vm((8, 1024, 128), BF),
            vm((4, 8, 32, 128), BF),
            vm((4, 8, 32, 128), BF),
            vm((32, 8, 128), BF),
            vm((32, 8, 128), BF),
            vm((8, 32, 128), BF),
            vm((4, 2, 32, 128), BF),
            vm((4, 2, 32, 128), BF),
            vm((8, 32, 128), BF),
            vm((2, 2, 256, 128), BF),
            vm((32, 2, 8, 128), BF),
            vm((2, 32, 8, 128), BF),
            pltpu.SemaphoreType.DMA((15,)),
            pltpu.SemaphoreType.DMA((15,)),
        ],
        compiler_params=pltpu.CompilerParams(
            collective_id=0, has_side_effects=True, vmem_limit_bytes=56 * 2**20
        ),
    )(*operands)
    return msa.reshape(64, 8, 128), pair


def solution(mesh):
    return jax.shard_map(
        shards,
        mesh=mesh,
        in_specs=(
            P("seq", "row", None),
            P("seq", "row", None),
            P(),
            P(),
            P(),
            P(),
            P(),
            P(),
            P(),
            P(),
            P(None, "seq", None),
            P("seq", None),
            P("seq"),
            P(None, "seq"),
            P(),
            P("seq", None),
            P(None, "seq"),
        ),
        out_specs=(P("seq", "row", "branch"), P("seq", "row", "branch")),
        check_vma=False,
    )
```

time: 238 us -> 75.3 us (0.32)
  blocking collectives: 132 us -> 0 us
  Pallas kernels: 0 us -> 65.2 us
  starting transfers between devices: 46 us -> 0 us
  between operations: 15.4 us -> 0.69 us
  waiting for transfers between devices: 12.3 us -> 0 us
  matrix products: 8.93 us -> 0 us
  other arithmetic: 7.29 us -> 0.59 us
  local copies, waits for them, and re-layouts: 14.9 us -> 8.57 us
    all_gather x5 -> x0, blocking collectives: 122 us -> none  [the longest x1 44.8 us: shards(): right = lax.all_gather(right, 'row', axis=0, tiled=True)]
    pallas_call x0 -> x1, Pallas kernels: none -> 65.2 us  [shards(): pl.pallas_call(body, out_shape=(jax.ShapeDtypeStruct((2, NR, 8, 128), BF)...]
    all_to_all x6 -> x0, starting transfers between devices: 44.4 us -> none  [the longest x1 13.6 us: shards(): got = lax.all_to_all(sent, 'row', split_axis=0, concat_axis=0, tiled=True)]
    unnamed x1 -> x0, blocking collectives: 9.69 us -> none
    dot_general x16 -> x0, matrix products: 8.93 us -> none  [the longest x7 4.36 us: mm(): return jnp.dot(a, b, preferred_element_type=F32)]
    all_to_all x6 -> x0, waiting for transfers between devices: 8.89 us -> none  [the longest x1 8.88 us: shards(): lax.all_to_all(mixed, 'row', split_axis=1, concat_axis=0, tiled=True)]
    reduce_sum x10 -> x0, other arithmetic: 3.46 us -> none  [the longest x5 1.67 us: layer_normalize(): spread = jnp.mean(centred * centred, axis=axis, keepdims=True)]
    ppermute x1 -> x0, waiting for transfers between devices: 3.36 us -> none  [shards(): other = lax.ppermute(mixed, 'branch', [(i, i ^ 1) for i in range(nb)])]
  transfers between devices with their start and end apart: 8 -> 0, of which waited for: 2 -> 0; matrix products, arithmetic and copies ran while one was open for 10% -> 0% of each run, Pallas kernels for 0% -> 0%
where the time goes in v3:
time: 75.3 us; the launch traced here: 75.1 us
  Pallas kernels  65.2 us (87%)
  local copies, waits for them, and re-layouts  8.57 us (11%)
    pallas_call x1, Pallas kernels, shards(): pl.pallas_call(body, out_shape=(jax.ShapeDtypeStruct((2, NR, 8, 128), BF)...  65.2 us
    unnamed x21, local copies, waits for them, and re-layouts  5.51 us

profile of v3, /device:TPU:1, one launch (start us, length us, event | category | flops | bytes accessed | tf_op | source)
XLA Modules:
  0.0 75.1 jit_solution(13946999573453530858)
XLA Ops:
  0.6 0.0 copy-start
  0.6 1.0 %copy-done = bf16[256,4,256]{2,1,0:T(4,128)(2,1)S(1)} copy-done((bf16[256,4,256]{2,1,0:T(4,128)(2,1)S(1)}, bf16[256,4,256]{2,1,0:T(4,128)(2,1)}, u32[]{:S(2)}) %copy-start) | copy-done | bytes 524312
  1.7 0.1 constant_dynamic-slice_fusion
  1.8 0.0 copy-start.3
  1.8 0.7 copy.40
  2.5 0.0 copy-start.1
  2.5 0.0 copy-done.3
  2.5 0.6 slice_bitcast_fusion
  3.1 0.8 %copy.34.ol_ref = bf16[256,256]{1,0:T(8,128)(2,1)} copy(bf16[256,256]{0,1:T(8,128)(2,1)S(1)} %bitcast.24) | data formatting | bytes 262144 | tf_op jit(solution)/shard_map/tile | solution.py:370
  3.9 0.0 copy-done.1
  3.9 0.1 copy.33
  4.0 0.8 %copy.35.oo_ref = bf16[128,1024]{1,0:T(8,128)(2,1)} copy(bf16[128,1024]{0,1:T(8,128)(2,1)S(1)} %bitcast.23) | data formatting | bytes 524288 | tf_op jit(solution)/shard_map/reshape | solution.py:372
  4.9 0.7 copy-done.6
  5.5 0.0 copy-done.7
  5.5 0.7 copy.36.col_ref
  6.3 0.0 copy-done.4
  6.3 0.7 copy.37.to_ref
  7.0 0.0 copy-done.5
  7.0 0.6 convert_bitcast_fusion.bm_ref
  7.6 65.2 %shard_map.176 = (bf16[2,32,8,128]{3,2,1,0:T(8,128)(2,1)}, bf16[32,8,128]{2,1,0:T(8,128)(2,1)}) custom-call(bf16[2,32,8,256]{3,2,1,0:T(8,128)(2,1)} %bitcast.25, bf16[32,8,256]{2,1,0:T(8,128)(2,1)} %p_ref.1, f32[1,256]{1,0:T(1,128)} %bitcast.27, f32[1,256]{1,0:T(1,128)} %bitcast.28, bf16[4,256,128]{2,1,0:T(8,128)(2,1)} %bitcast.22, bf16[256,256]{1,0:T(8,128)(2,1)} %mw_ref.1, ...), custom_call_target="tpu_custom_call" | custom-call | tf_op jit(solution)/shard_map/pallas_call | solution.py:383
  72.8 0.0 copy-start.2
  72.8 1.6 %copy.43 = bf16[64,8,128]{2,1,0:T(8,128)(2,1)} copy(bf16[64,8,128]{2,1,0:T(8,128)(2,1)} %bitcast.26) | data formatting | bytes 262144
  74.4 0.0 copy-done.2
  74.4 0.6 copy.44
  (6 shorter events, 0.0 us)
Async XLA Ops:
  0.6 1.0 %copy-start = (bf16[256,4,256]{2,1,0:T(4,128)(2,1)S(1)}, bf16[256,4,256]{2,1,0:T(4,128)(2,1)}, u32[]{:S(2)}) copy-start(bf16[256,4,256]{2,1,0:T(4,128)(2,1)} %param.21) | copy-start | bytes 1572868
  1.8 0.8 %copy-start.3 = (bf16[256,2,32]{0,2,1:T(8,128)(2,1)S(1)}, bf16[256,2,32]{0,2,1:T(8,128)(2,1)}, u32[]{:S(2)}) copy-start(bf16[256,2,32]{0,2,1:T(8,128)(2,1)} %param.23) | copy-start | bytes 98308
  2.5 1.4 %copy-start.1 = (bf16[32,32,128]{2,1,0:T(8,128)(2,1)S(1)}, bf16[32,32,128]{2,1,0:T(8,128)(2,1)}, u32[]{:S(2)}) copy-start(bf16[32,32,128]{2,1,0:T(8,128)(2,1)} %param.24) | copy-start | bytes 786436
  4.9 0.7 copy-start.6
  4.9 0.7 copy-start.7
  5.5 0.7 copy-start.4
  6.3 0.7 copy-start.5
  72.8 1.6 %copy-start.2 = (bf16[32,8,128]{2,1,0:T(8,128)(2,1)S(1)}, bf16[32,8,128]{2,1,0:T(8,128)(2,1)}, u32[]{:S(2)}) copy-start(bf16[32,8,128]{2,1,0:T(8,128)(2,1)} %get-tuple-element.11) | copy-start | bytes 196612

commit v4 on v3

v4 whole, which is shorter than its diff:
```python
import jax
import jax.numpy as jnp
from jax import lax
from jax.experimental import pallas as pl
from jax.experimental.pallas import tpu as pltpu
from jax.sharding import PartitionSpec as P

EPSILON = 1e-05
BF = jnp.bfloat16
F32 = jnp.float32
NZ, NW = 8, 4
NR = NZ * NW
NQ = 4


def mm(a, b):
    return jnp.dot(a, b, preferred_element_type=F32)


def mm_t(a, b):
    return lax.dot_general(a, b, (((1,), (1,)), ((), ())), preferred_element_type=F32)


def normalize(x, axis):
    average = jnp.mean(x, axis=axis, keepdims=True)
    centred = x - average
    spread = jnp.mean(centred * centred, axis=axis, keepdims=True)
    return centred * lax.rsqrt(spread + EPSILON)


def column(row):
    n = row.shape[1]
    eye = lax.broadcasted_iota(jnp.int32, (n, n), 0) == lax.broadcasted_iota(
        jnp.int32, (n, n), 1
    )
    return jnp.sum(jnp.where(eye, row, 0.0), axis=1, keepdims=True)


def body(
    a_hbm,
    p_hbm,
    ag_hbm,
    pg_hbm,
    aw_hbm,
    mw_hbm,
    oi_hbm,
    oo_hbm,
    bm_hbm,
    cg_hbm,
    ti_hbm,
    tg_hbm,
    tn_hbm,
    to_hbm,
    cn_hbm,
    up_hbm,
    dn_hbm,
    msa_ref,
    pair_ref,
    a_ref,
    p_ref,
    ag_ref,
    pg_ref,
    aw_ref,
    mw_ref,
    oi_ref,
    oo_ref,
    bm_ref,
    cg_ref,
    ti_ref,
    tg_ref,
    tn_ref,
    to_ref,
    cn_ref,
    up_ref,
    dn_ref,
    awf,
    awt,
    oot,
    g,
    w,
    tin,
    lt,
    rt,
    ls,
    rs,
    bs,
    lb,
    rb,
    bf,
    mn,
    lx,
    lxt,
    qkv,
    rg,
    rgt,
    pq,
    ob,
    orb,
    tb,
    bk,
    xs,
    xr,
    pn,
    fb,
    mx,
    ao,
    mo,
    cs,
    ss,
    rv,
):
    b = lax.axis_index("branch")
    r = lax.axis_index("row")
    q = lax.axis_index("seq")
    zi = r // NW
    wi = r % NW
    inside = (r // (NR // 2)) == b
    cols = pl.ds(pl.multiple_of(b * 128, 128), 128)

    loads = {}
    for n, (src, dst) in enumerate(
        (
            (p_hbm, p_ref),
            (a_hbm, a_ref),
            (tg_hbm, tg_ref),
            (tn_hbm, tn_ref),
            (to_hbm, to_ref),
            (up_hbm, up_ref),
            (dn_hbm, dn_ref),
            (pg_hbm, pg_ref),
            (oi_hbm, oi_ref),
            (aw_hbm.at[:, :, cols], aw_ref),
            (oo_hbm, oo_ref),
            (bm_hbm, bm_ref),
            (cg_hbm, cg_ref),
            (ti_hbm, ti_ref),
            (ag_hbm, ag_ref),
            (cn_hbm, cn_ref),
            (mw_hbm.at[:, cols], mw_ref),
        )
    ):
        loads[n] = pltpu.make_async_copy(src, dst, cs.at[n])
        loads[n].start()

    def signal(where):
        pl.semaphore_signal(
            barrier, inc=1, device_id=where, device_id_type=pl.DeviceIdType.MESH
        )

    def send(src, dst, k, where):
        pltpu.make_async_remote_copy(
            src_ref=src,
            dst_ref=dst,
            send_sem=ss.at[k],
            recv_sem=rv.at[k],
            device_id=where,
            device_id_type=pl.DeviceIdType.MESH,
        ).start()

    def arrived(view, k):
        pltpu.make_async_copy(view, view, rv.at[k]).wait()

    def left_here(view, k):
        pltpu.make_async_copy(view, view, ss.at[k]).wait()

    def row_peers(do):
        def step(k, carry):
            do(lax.rem(r + k, NR))
            return carry

        lax.fori_loop(1, NR, step, 0)

    barrier = pltpu.get_barrier_semaphore()
    row_peers(lambda peer: signal({"row": peer}))
    for k in range(1, NQ):
        signal({"seq": lax.rem(q + k, NQ)})
    signal({"branch": 1 - b})

    loads[0].wait()
    g[q] = jnp.transpose(p_ref[...].astype(F32), (1, 0, 2)).astype(BF)
    loads[1].wait()

    pl.semaphore_wait(barrier, NR - 1 + NQ - 1 + 1)

    for k in range(1, NQ):
        send(g.at[q], g.at[q], 0, {"seq": lax.rem(q + k, NQ)})
    row_peers(lambda peer: send(a_ref.at[:, peer], mn.at[r], 1, {"row": peer}))

    for s in range(2):
        mn[r, s] = a_ref[s, r]
    for n in range(2, 7):
        loads[n].wait()
    w[q, 0:32] = tg_ref[...]
    w[q, 32:64] = (to_ref[...].astype(F32) * column(tn_ref[...])).astype(BF)
    w[q, 64:192] = up_ref[...]
    w[q, 192:320] = dn_ref[...]
    loads[7].wait()
    loads[8].wait()
    lane = lax.broadcasted_iota(jnp.int32, (16, 8, 256), 2) // 32
    sub = lax.broadcasted_iota(jnp.int32, (16, 8, 256), 1)
    wide_left = jnp.concatenate([oi_ref[0]] * 8, axis=0)
    for s in range(2):
        for k in range(2):
            x = a_ref[s, 16 * k : 16 * k + 16].astype(F32).reshape(128, 256)
            x = (normalize(x, 1) * pg_ref[...]).astype(BF)
            x = mm_t(x, wide_left).reshape(16, 8, 256)
            lx[32 * s + 16 * k : 32 * s + 16 * k + 16] = jnp.sum(
                jnp.where(lane == sub, x, 0.0), axis=1
            )
    lxt[...] = jnp.transpose(lx[...]).astype(BF)
    loads[9].wait()
    awf[...] = aw_ref[...].astype(F32).reshape(1024, 128)
    for t in range(4):
        awt[t] = awf[pl.ds(t, 256, stride=4)].astype(BF)
    loads[10].wait()
    x = jnp.transpose(oo_ref[...].astype(F32), (1, 0, 2)).reshape(1024, 128)
    oot[...] = jnp.transpose(x).astype(BF)
    for n in range(11, 17):
        loads[n].wait()

    head_row = lax.broadcasted_iota(jnp.int32, (8, 128), 0)
    pick = jnp.where(head_row == NQ * b + q, bm_ref[...].astype(F32), 0.0)
    pick = jnp.sum(pick, axis=0, keepdims=True)
    pair_gain = column(cg_ref[...])
    arrived(g.at[pl.ds(0, NQ - 1)], 0)

    def bias_row(i, acc):
        unit = normalize(g[:, i].astype(F32).reshape(128, 256), 0)
        tin[i] = (unit * pair_gain).astype(BF)
        return acc + mm(jnp.where(head_row == i, pick, 0.0).astype(BF), unit.astype(BF))

    bs[...] = lax.fori_loop(0, 8, bias_row, jnp.zeros((8, 256), F32)).astype(BF)
    bf[q, r] = bs[...]
    for dz in range(NZ):
        for dw in range(NW):
            if dz or dw:
                peer = lax.rem(zi + dz, NZ) * NW + lax.rem(wi + dw, NW)
                send(bs, bf.at[q, r], 17 + dz, {"row": peer})

    def tri_row_step(i, carry):
        lin = mm(ti_ref[...].reshape(128, 128), tin[i])
        lt[i] = lin[0:32] * jax.nn.sigmoid(lin[32:64])
        rt[i] = lin[64:96] * jax.nn.sigmoid(lin[96:128])
        return carry

    lax.fori_loop(0, 8, tri_row_step, 0)
    ls[...] = jnp.transpose(lt[...], (1, 0, 2)).astype(BF)
    rs[...] = jnp.transpose(rt[...], (1, 0, 2)).astype(BF)
    lb[r] = ls[r]
    row_peers(lambda peer: send(ls.at[peer], lb.at[r], 3, {"row": peer}))

    @pl.when(inside)
    def _():
        rb[r % (NR // 2)] = rs[r]
        row_peers(lambda peer: send(rs.at[peer], rb.at[r % (NR // 2)], 4, {"row": peer}))

    for k in range(1, NQ):
        send(w.at[q], w.at[q], 2, {"seq": lax.rem(q + k, NQ)})

    arrived(mn.at[pl.ds(0, NR - 1)], 1)
    for s in range(2):
        x = normalize(mn[:, s].astype(F32).reshape(256, 256), 1)
        right = mm_t(oi_ref[1], (x * pg_ref[...]).astype(BF))
        rg[zi, wi, s] = jnp.where(b == 0, right[:, :128], right[:, 128:]).astype(BF)
        normed = (x * ag_ref[...]).astype(BF)
        qkv[s, 0] = (mm(normed, awt[0]) * (32.0**-0.5)).astype(BF)
        qkv[s, 1] = mm(normed, awt[1]).astype(BF)
        qkv[s, 2] = mm(normed, awt[2]).astype(BF)
        qkv[s, 3] = jax.nn.sigmoid(mm(normed, awt[3])).astype(BF)

    def z_peers(k, carry):
        send(rg.at[zi, wi], rg.at[zi, wi], 8, {"row": lax.rem(zi + k, NZ) * NW + wi})
        return carry

    lax.fori_loop(1, NZ, z_peers, 0)

    for dz in (0, 1, 7, 2, 6, 3, 5, 4):
        arrived(bf.at[0, pl.ds(0, NW if dz else NW - 1)], 17 + dz)
        part = bf.at[q, pl.ds(lax.rem(zi + NZ - dz, NZ) * NW, NW)]
        for k in range(1, NQ):
            send(part, part, 24 + k, {"seq": lax.rem(q + k, NQ)})

    arrived(lb.at[pl.ds(0, NR - 1)], 3)

    @pl.when(inside)
    def _():
        arrived(rb.at[pl.ds(0, NR // 2 - 1)], 4)

    @pl.when(jnp.logical_not(inside))
    def _():
        arrived(rb, 4)

    tl = lb[...].astype(F32).reshape(256, 256).astype(BF)
    tr = rb[...].astype(F32).reshape(128, 256).astype(BF)
    tb[...] = mm_t(tl, tr).reshape(32, 8, 128).astype(BF)
    bk[r] = tb[r]
    row_peers(lambda peer: send(tb.at[peer], bk.at[r], 6, {"row": peer}))

    arrived(rg.at[pl.ds(0, NZ - 1), 0], 8)
    for k in range(1, NW):
        send(rg.at[:, wi], rg.at[:, wi], 9, {"row": zi * NW + lax.rem(wi + k, NW)})

    lane_head = lax.broadcasted_iota(jnp.int32, (256, 128), 1) // 32
    for s in range(2):
        value = jnp.zeros((256, 128), F32)
        for k in range(NQ):
            h = lax.rem(q + NQ - k, NQ)
            if s == 0 and k:
                arrived(bf.at[0], 24 + k)
            here = lane_head == h
            query = jnp.where(here, qkv[s, 0].astype(F32), 0.0).astype(BF)
            score = mm_t(query, qkv[s, 1]) + bf[h].astype(F32).reshape(256, 256)
            expo = jnp.exp(score - jnp.max(score, axis=1, keepdims=True))
            total = jnp.sum(expo, axis=1, keepdims=True)
            value = jnp.where(here, mm(expo.astype(BF), qkv[s, 2]) / total, value)
        mx[b, s] = (qkv[s, 3].astype(F32) * value).astype(BF)
        send(mx.at[b, s], mx.at[b, s], 13 + s, {"branch": 1 - b})

    arrived(rg.at[:, pl.ds(0, NW - 1)], 9)
    for s in range(2):
        x = rg[:, :, s].astype(F32).reshape(32, 32, 128)
        x = jnp.transpose(x, (1, 0, 2)).astype(BF)
        for d in range(32):
            rgt[32 * s : 32 * s + 32, 128 * d : 128 * d + 128] = x[d]

    def outer_step(n, carry):
        x = mm(lxt[...], rgt[:, pl.ds(pl.multiple_of(n * 256, 256), 256)]).astype(BF)
        for d in range(2):
            for i in range(8):
                pq[
                    i // 2,
                    pl.ds(pl.multiple_of(n * 64 + 32 * d, 32), 32),
                    128 * (i % 2) : 128 * (i % 2) + 128,
                ] = x[32 * i : 32 * i + 32, 128 * d : 128 * d + 128]
        return carry

    lax.fori_loop(0, 16, outer_step, 0)

    arrived(bk.at[pl.ds(0, NR - 1)], 6)
    xs[...] = jnp.transpose(bk[...].astype(F32), (1, 0, 2)).astype(BF)
    xr[q] = xs[pl.ds(2 * q, 2)]
    for k in range(1, NQ):
        peer = lax.rem(q + k, NQ)
        send(xs.at[pl.ds(2 * peer, 2)], xr.at[q], 10, {"seq": peer})

    for s in range(2):
        arrived(mx.at[0, s], 13 + s)
        x = mm(mx[0, s], mw_ref[0:128]) + mm(mx[1, s], mw_ref[128:256])
        x = mn[:, s, :, cols].astype(F32).reshape(256, 128) + x
        ao[:, s] = x.reshape(32, 8, 128).astype(BF)
        mo[s, r] = ao[r, s]
        row_peers(lambda peer: send(ao.at[peer, s], mo.at[s, r], 15 + s, {"row": peer}))

    for n in range(4):
        x = (mm(oot[...], pq[n]) * (1.0 / 256.0)).astype(BF)
        for i in range(2):
            ob[:, 2 * n + i] = x[:, 128 * i : 128 * i + 128].reshape(4, 32, 128)
    orb[q] = ob[q]
    for k in range(1, NQ):
        peer = lax.rem(q + k, NQ)
        send(ob.at[peer], orb.at[q], 12, {"seq": peer})

    arrived(w.at[pl.ds(0, NQ - 1)], 2)
    out_w = w[:, 32:64].astype(F32).reshape(128, 128)
    out_w = jnp.transpose(out_w).astype(BF)
    trans_gain = column(cn_ref[...])
    pair_in = jnp.concatenate(
        [g[:, 2 * q + i, :, cols].astype(F32).reshape(128, 128) for i in range(2)], axis=1
    )
    tri_row = jnp.concatenate([tin[2 * q + i, :, cols] for i in range(2)], axis=1)
    gate = jax.nn.sigmoid(mm(w[:, 0:32].reshape(128, 128), tri_row))
    arrived(xr.at[pl.ds(0, NQ - 1)], 10)
    row_tri = jnp.concatenate(
        [xr[:, i].astype(F32).reshape(128, 128) for i in range(2)], axis=1
    )
    first = pair_in + gate * mm(out_w, normalize(row_tri, 0).astype(BF))
    first = first.astype(BF).astype(F32)
    trans = (normalize(first, 0) * trans_gain).astype(BF)
    moved = first
    for k in range(NQ):
        hidden = jnp.maximum(mm(w[k, 64:192], trans), 0.0).astype(BF)
        moved = moved + mm(w[k, 192:320], hidden)
    moved = moved.astype(BF)
    for i in range(2):
        pn[:, i] = moved[:, 128 * i : 128 * i + 128].reshape(4, 32, 128)
    fb[pl.ds(2 * q, 2)] = pn[q]
    for k in range(1, NQ):
        peer = lax.rem(q + k, NQ)
        send(pn.at[peer], fb.at[pl.ds(2 * q, 2)], 11, {"seq": peer})

    arrived(orb.at[pl.ds(0, NQ - 1)], 12)
    update = orb[0].astype(F32)
    for k in range(1, NQ):
        update = update + orb[k].astype(F32)
    update = update.astype(BF).astype(F32)
    arrived(fb.at[pl.ds(0, 6)], 11)
    update = update + fb[...].astype(F32)
    pair_ref[...] = jnp.transpose(update, (1, 0, 2)).reshape(256, 128).astype(BF)

    for s in range(2):
        arrived(mo.at[s, pl.ds(0, NR - 1)], 15 + s)
        msa_ref[256 * s : 256 * s + 256] = mo[s].astype(F32).reshape(256, 128).astype(BF)

    for k, view in (
        (0, g.at[pl.ds(0, NQ - 1)]),
        (1, mn.at[pl.ds(0, NR - 1)]),
        (2, w.at[pl.ds(0, NQ - 1)]),
        (3, lb.at[pl.ds(0, NR - 1)]),
        (6, bk.at[pl.ds(0, NR - 1)]),
        (8, rg.at[pl.ds(0, NZ - 1), 0]),
        (9, rg.at[:, pl.ds(0, NW - 1)]),
        (10, xr.at[pl.ds(0, NQ - 1)]),
        (11, fb.at[pl.ds(0, 6)]),
        (12, orb.at[pl.ds(0, NQ - 1)]),
        (13, mx.at[0, 0]),
        (14, mx.at[0, 0]),
        (15, mo.at[0, pl.ds(0, NR - 1)]),
        (16, mo.at[0, pl.ds(0, NR - 1)]),
        (17, bf.at[0, pl.ds(0, NW - 1)]),
    ):
        left_here(view, k)
    for dz in range(1, NZ):
        left_here(bf.at[0, pl.ds(0, NW)], 17 + dz)
    for k in range(1, NQ):
        left_here(bf.at[0], 24 + k)

    @pl.when(inside)
    def _():
        left_here(lb.at[pl.ds(0, NR - 1)], 4)


def shards(
    alignment_input,
    pairwise_input,
    alignment_gain,
    product_gain,
    attention_weight,
    mixing_weight,
    outer_input_weight,
    outer_output_weight,
    bias_matrix,
    pairwise_gain,
    triangle_input_weight,
    triangle_gate_weight,
    triangle_gain,
    triangle_output_weight,
    transition_gain,
    transition_up_weight,
    transition_down_weight,
):
    operands = (
        alignment_input.reshape(2, NR, 8, 256),
        pairwise_input,
        alignment_gain.reshape(1, 256),
        product_gain.reshape(1, 256),
        attention_weight,
        mixing_weight,
        outer_input_weight.transpose(1, 2, 0),
        outer_output_weight,
        bias_matrix.T,
        pairwise_gain.reshape(1, 128),
        triangle_input_weight,
        triangle_gate_weight,
        triangle_gain.reshape(1, 32),
        triangle_output_weight.T,
        transition_gain.reshape(1, 128),
        transition_up_weight,
        transition_down_weight,
    )
    vm = pltpu.VMEM
    held = [vm(x.shape, x.dtype) for x in operands]
    held[4] = vm((256, 4, 128), BF)
    held[5] = vm((256, 128), BF)
    msa, pair = pl.pallas_call(
        body,
        out_shape=(
            jax.ShapeDtypeStruct((512, 128), BF),
            jax.ShapeDtypeStruct((256, 128), BF),
        ),
        in_specs=[pl.BlockSpec(memory_space=pltpu.HBM)] * len(operands),
        out_specs=[pl.BlockSpec(memory_space=pltpu.VMEM)] * 2,
        scratch_shapes=held
        + [
            vm((1024, 128), F32),
            vm((4, 256, 128), BF),
            vm((128, 1024), BF),
            vm((4, 8, 32, 256), BF),
            vm((4, 320, 128), BF),
            vm((8, 128, 256), BF),
            vm((8, 32, 256), F32),
            vm((8, 32, 256), F32),
            vm((32, 8, 256), BF),
            vm((32, 8, 256), BF),
            vm((8, 256), BF),
            vm((32, 8, 256), BF),
            vm((16, 8, 256), BF),
            vm((4, 32, 8, 256), BF),
            vm((32, 2, 8, 256), BF),
            vm((64, 256), F32),
            vm((256, 64), BF),
            vm((2, 4, 256, 128), BF),
            vm((8, 4, 2, 32, 128), BF),
            vm((64, 4096), BF),
            vm((4, 1024, 256), BF),
            vm((4, 8, 32, 128), BF),
            vm((4, 8, 32, 128), BF),
            vm((32, 8, 128), BF),
            vm((32, 8, 128), BF),
            vm((8, 32, 128), BF),
            vm((4, 2, 32, 128), BF),
            vm((4, 2, 32, 128), BF),
            vm((8, 32, 128), BF),
            vm((2, 2, 256, 128), BF),
            vm((32, 2, 8, 128), BF),
            vm((2, 32, 8, 128), BF),
            pltpu.SemaphoreType.DMA((17,)),
            pltpu.SemaphoreType.DMA((28,)),
            pltpu.SemaphoreType.DMA((28,)),
        ],
        compiler_params=pltpu.CompilerParams(
            collective_id=0, has_side_effects=True, vmem_limit_bytes=67_043_328
        ),
    )(*operands)
    return msa.reshape(64, 8, 128), pair.reshape(32, 8, 128)


def solution(mesh):
    return jax.shard_map(
        shards,
        mesh=mesh,
        in_specs=(
            P("seq", "row", None),
            P("seq", "row", None),
            P(),
            P(),
            P(),
            P(),
            P(),
            P(),
            P(),
            P(),
            P(None, "seq", None),
            P("seq", None),
            P("seq"),
            P(None, "seq"),
            P(),
            P("seq", None),
            P(None, "seq"),
        ),
        out_specs=(P("seq", "row", "branch"), P("seq", "row", "branch")),
        check_vma=False,
    )
```

time: 75.3 us -> 59.1 us (0.78)
  Pallas kernels: 65.2 us -> 56.1 us
  local copies, waits for them, and re-layouts: 8.57 us -> 2.23 us
    pallas_call x1, Pallas kernels: 65.2 us -> 56.1 us  [shards(): pl.pallas_call(body, out_shape=(jax.ShapeDtypeStruct((512, 128), BF), jax...]
    unnamed x21 -> x4, local copies, waits for them, and re-layouts: 5.51 us -> 2.23 us
    another operation x3 -> x0, local copies, waits for them, and re-layouts: 1.51 us -> none  [the longest x2 0.77 us: shards(): jnp.tile(outer_input_weight[:, 0], (1, 8))]
    reshape x1 -> x0, local copies, waits for them, and re-layouts: 0.85 us -> none  [shards(): outer_output_weight.transpose(2, 1, 0).reshape(128, 1024)]
where the time goes in v4:
time: 59.1 us; the launch traced here: 59 us
  Pallas kernels  56.1 us (95%)
  local copies, waits for them, and re-layouts  2.23 us (4%)
  between operations  0.65 us (1%)
    pallas_call x1, Pallas kernels, shards(): pl.pallas_call(body, out_shape=(jax.ShapeDtypeStruct((512, 128), BF), jax...  56.1 us
    unnamed x4, local copies, waits for them, and re-layouts  2.23 us

profile of v4, /device:TPU:1, one launch (start us, length us, event | category | flops | bytes accessed | tf_op | source)
XLA Modules:
  0.0 59.0 jit_solution(10944867240011963285)
XLA Ops:
  0.6 56.1 %shard_map.176 = (bf16[512,128]{1,0:T(8,128)(2,1)}, bf16[256,128]{1,0:T(8,128)(2,1)}) custom-call(bf16[2,32,8,256]{3,2,1,0:T(8,128)(2,1)} %bitcast.11, bf16[32,8,256]{2,1,0:T(8,128)(2,1)} %p_hbm.1, f32[1,256]{1,0:T(1,128)} %bitcast.17, f32[1,256]{1,0:T(1,128)} %bitcast.18, bf16[256,4,256]{2,1,0:T(4,128)(2,1)} %aw_hbm.1, bf16[256,256]{1,0:T(8,128)(2,1)} %mw_hbm.1, ...), custom_call_target="tpu_custom_call" | custom-call | tf_op jit(solution)/shard_map/pallas_call | solution.py:474
  56.7 0.0 copy-start
  56.7 1.6 %copy.21 = bf16[64,8,128]{2,1,0:T(8,128)(2,1)} copy(bf16[64,8,128]{2,1,0:T(8,128)(2,1)} %bitcast.12) | data formatting | bytes 262144
  58.3 0.0 copy-done
  58.3 0.6 %copy.22 = bf16[32,8,128]{2,1,0:T(8,128)(2,1)} copy(bf16[32,8,128]{2,1,0:T(8,128)(2,1)S(1)} %bitcast.13) | data formatting | bytes 131072
Async XLA Ops:
  56.7 1.6 %copy-start = (bf16[256,128]{1,0:T(8,128)(2,1)S(1)}, bf16[256,128]{1,0:T(8,128)(2,1)}, u32[]{:S(2)}) copy-start(bf16[256,128]{1,0:T(8,128)(2,1)} %get-tuple-element.5) | copy-start | bytes 196612

commit v5 on v4

--- a/solution.py
+++ b/solution.py
@@ -88,6 +88,7 @@
     rb,
     bf,
     mn,
+    nm,
     lx,
     lxt,
     qkv,
@@ -163,6 +164,28 @@
     def left_here(view, k):
         pltpu.make_async_copy(view, view, ss.at[k]).wait()
 
+    right_nb = {"seq": lax.rem(q + 1, NQ)}
+    left_nb = {"seq": lax.rem(q + NQ - 1, NQ)}
+    q_right = lax.rem(q + 1, NQ)
+    q_left = lax.rem(q + NQ - 1, NQ)
+
+    def both_ways(view, k):
+        for c in range(2):
+            send(view(q, c), view(q, c), k + c, right_nb)
+            send(view(q, c), view(q, c), k + 2 + c, left_nb)
+
+    def pass_on(view, k):
+        arrived(view(q, 0), k)
+        send(view(q_left, 0), view(q_left, 0), k + 4, right_nb)
+        arrived(view(q, 1), k + 3)
+        send(view(q_right, 1), view(q_right, 1), k + 5, left_nb)
+
+    def g_part(slot, c):
+        return g.at[slot, pl.ds(4 * c, 4)]
+
+    def w_part(slot, c):
+        return w.at[slot, pl.ds(160 * c, 160)]
+
     def row_peers(do):
         def step(k, carry):
             do(lax.rem(r + k, NR))
@@ -182,9 +205,8 @@
 
     pl.semaphore_wait(barrier, NR - 1 + NQ - 1 + 1)
 
-    for k in range(1, NQ):
-        send(g.at[q], g.at[q], 0, {"seq": lax.rem(q + k, NQ)})
-    row_peers(lambda peer: send(a_ref.at[:, peer], mn.at[r], 1, {"row": peer}))
+    both_ways(g_part, 0)
+    row_peers(lambda peer: send(a_ref.at[:, peer], mn.at[r], 12, {"row": peer}))
 
     for s in range(2):
         mn[r, s] = a_ref[s, r]
@@ -194,6 +216,7 @@
     w[q, 32:64] = (to_ref[...].astype(F32) * column(tn_ref[...])).astype(BF)
     w[q, 64:192] = up_ref[...]
     w[q, 192:320] = dn_ref[...]
+    pass_on(g_part, 0)
     loads[7].wait()
     loads[8].wait()
     lane = lax.broadcasted_iota(jnp.int32, (16, 8, 256), 2) // 32
@@ -222,20 +245,25 @@
     pick = jnp.where(head_row == NQ * b + q, bm_ref[...].astype(F32), 0.0)
     pick = jnp.sum(pick, axis=0, keepdims=True)
     pair_gain = column(cg_ref[...])
-    arrived(g.at[pl.ds(0, NQ - 1)], 0)
 
     def bias_row(i, acc):
         unit = normalize(g[:, i].astype(F32).reshape(128, 256), 0)
         tin[i] = (unit * pair_gain).astype(BF)
         return acc + mm(jnp.where(head_row == i, pick, 0.0).astype(BF), unit.astype(BF))
 
-    bs[...] = lax.fori_loop(0, 8, bias_row, jnp.zeros((8, 256), F32)).astype(BF)
+    arrived(g_part(q, 0), 2)
+    arrived(g_part(q, 0), 4)
+    acc = lax.fori_loop(0, 4, bias_row, jnp.zeros((8, 256), F32))
+    arrived(g_part(q, 1), 1)
+    arrived(g_part(q, 1), 5)
+    bs[...] = lax.fori_loop(4, 8, bias_row, acc).astype(BF)
     bf[q, r] = bs[...]
     for dz in range(NZ):
         for dw in range(NW):
             if dz or dw:
                 peer = lax.rem(zi + dz, NZ) * NW + lax.rem(wi + dw, NW)
-                send(bs, bf.at[q, r], 17 + dz, {"row": peer})
+                send(bs, bf.at[q, r], 13 + dz, {"row": peer})
+    both_ways(w_part, 6)
 
     def tri_row_step(i, carry):
         lin = mm(ti_ref[...].reshape(128, 128), tin[i])
@@ -247,66 +275,81 @@
     ls[...] = jnp.transpose(lt[...], (1, 0, 2)).astype(BF)
     rs[...] = jnp.transpose(rt[...], (1, 0, 2)).astype(BF)
     lb[r] = ls[r]
-    row_peers(lambda peer: send(ls.at[peer], lb.at[r], 3, {"row": peer}))
+    row_peers(lambda peer: send(ls.at[peer], lb.at[r], 33, {"row": peer}))
 
     @pl.when(inside)
     def _():
         rb[r % (NR // 2)] = rs[r]
-        row_peers(lambda peer: send(rs.at[peer], rb.at[r % (NR // 2)], 4, {"row": peer}))
-
-    for k in range(1, NQ):
-        send(w.at[q], w.at[q], 2, {"seq": lax.rem(q + k, NQ)})
-
-    arrived(mn.at[pl.ds(0, NR - 1)], 1)
+        row_peers(lambda peer: send(rs.at[peer], rb.at[r % (NR // 2)], 34, {"row": peer}))
+
+    arrived(mn.at[pl.ds(0, NR - 1)], 12)
     for s in range(2):
         x = normalize(mn[:, s].astype(F32).reshape(256, 256), 1)
         right = mm_t(oi_ref[1], (x * pg_ref[...]).astype(BF))
         rg[zi, wi, s] = jnp.where(b == 0, right[:, :128], right[:, 128:]).astype(BF)
-        normed = (x * ag_ref[...]).astype(BF)
-        qkv[s, 0] = (mm(normed, awt[0]) * (32.0**-0.5)).astype(BF)
-        qkv[s, 1] = mm(normed, awt[1]).astype(BF)
-        qkv[s, 2] = mm(normed, awt[2]).astype(BF)
-        qkv[s, 3] = jax.nn.sigmoid(mm(normed, awt[3])).astype(BF)
+        nm[s] = (x * ag_ref[...]).astype(BF)
 
     def z_peers(k, carry):
-        send(rg.at[zi, wi], rg.at[zi, wi], 8, {"row": lax.rem(zi + k, NZ) * NW + wi})
+        send(rg.at[zi, wi], rg.at[zi, wi], 35, {"row": lax.rem(zi + k, NZ) * NW + wi})
         return carry
 
     lax.fori_loop(1, NZ, z_peers, 0)
+    pass_on(w_part, 6)
+    for s in range(2):
+        qkv[s, 0] = (mm(nm[s], awt[0]) * (32.0**-0.5)).astype(BF)
+        qkv[s, 1] = mm(nm[s], awt[1]).astype(BF)
+        qkv[s, 2] = mm(nm[s], awt[2]).astype(BF)
+        qkv[s, 3] = jax.nn.sigmoid(mm(nm[s], awt[3])).astype(BF)
+
+    def group(slot, dz):
+        return bf.at[slot, pl.ds(lax.rem(zi + NZ - dz, NZ) * NW, NW)]
 
     for dz in (0, 1, 7, 2, 6, 3, 5, 4):
-        arrived(bf.at[0, pl.ds(0, NW if dz else NW - 1)], 17 + dz)
-        part = bf.at[q, pl.ds(lax.rem(zi + NZ - dz, NZ) * NW, NW)]
-        for k in range(1, NQ):
-            send(part, part, 24 + k, {"seq": lax.rem(q + k, NQ)})
-
-    arrived(lb.at[pl.ds(0, NR - 1)], 3)
+        arrived(bf.at[0, pl.ds(0, NW if dz else NW - 1)], 13 + dz)
+        part = group(q, dz)
+        send(part, part, 21 + dz if dz < 4 else 25, right_nb)
+        send(part, part, 33 - dz if dz >= 4 else 30, left_nb)
+    for n in range(4):
+        arrived(bf.at[0, pl.ds(0, NW)], 21 + n)
+        send(group(q_left, n), group(q_left, n), 31, right_nb)
+        arrived(bf.at[0, pl.ds(0, NW)], 26 + n)
+        send(group(q_right, 7 - n), group(q_right, 7 - n), 32, left_nb)
+
+    arrived(rg.at[pl.ds(0, NZ - 1), 0], 35)
+    w_core = wi + 1 - 2 * (wi % 2)
+    w_far = lax.rem(wi + 2, NW)
+    other_core = {"row": zi * NW + w_core}
+    send(rg.at[:, wi], rg.at[:, wi], 37, {"row": zi * NW + w_far})
+    send(rg.at[:, wi], rg.at[:, wi], 36, other_core)
+
+    arrived(lb.at[pl.ds(0, NR - 1)], 33)
 
     @pl.when(inside)
     def _():
-        arrived(rb.at[pl.ds(0, NR // 2 - 1)], 4)
+        arrived(rb.at[pl.ds(0, NR // 2 - 1)], 34)
 
     @pl.when(jnp.logical_not(inside))
     def _():
-        arrived(rb, 4)
+        arrived(rb, 34)
 
     tl = lb[...].astype(F32).reshape(256, 256).astype(BF)
     tr = rb[...].astype(F32).reshape(128, 256).astype(BF)
     tb[...] = mm_t(tl, tr).reshape(32, 8, 128).astype(BF)
     bk[r] = tb[r]
-    row_peers(lambda peer: send(tb.at[peer], bk.at[r], 6, {"row": peer}))
-
-    arrived(rg.at[pl.ds(0, NZ - 1), 0], 8)
-    for k in range(1, NW):
-        send(rg.at[:, wi], rg.at[:, wi], 9, {"row": zi * NW + lax.rem(wi + k, NW)})
+    row_peers(lambda peer: send(tb.at[peer], bk.at[r], 39, {"row": peer}))
 
     lane_head = lax.broadcasted_iota(jnp.int32, (256, 128), 1) // 32
     for s in range(2):
         value = jnp.zeros((256, 128), F32)
         for k in range(NQ):
-            h = lax.rem(q + NQ - k, NQ)
-            if s == 0 and k:
-                arrived(bf.at[0], 24 + k)
+            h = lax.rem(q + (0, 1, 3, 2)[k], NQ)
+            if s == 0 and k == 1:
+                arrived(bf.at[0, pl.ds(0, 4 * NW)], 30)
+            if s == 0 and k == 2:
+                arrived(bf.at[0, pl.ds(0, 4 * NW)], 25)
+            if s == 0 and k == 3:
+                arrived(bf.at[0, pl.ds(0, 4 * NW)], 31)
+                arrived(bf.at[0, pl.ds(0, 4 * NW)], 32)
             here = lane_head == h
             query = jnp.where(here, qkv[s, 0].astype(F32), 0.0).astype(BF)
             score = mm_t(query, qkv[s, 1]) + bf[h].astype(F32).reshape(256, 256)
@@ -314,9 +357,21 @@
             total = jnp.sum(expo, axis=1, keepdims=True)
             value = jnp.where(here, mm(expo.astype(BF), qkv[s, 2]) / total, value)
         mx[b, s] = (qkv[s, 3].astype(F32) * value).astype(BF)
-        send(mx.at[b, s], mx.at[b, s], 13 + s, {"branch": 1 - b})
-
-    arrived(rg.at[:, pl.ds(0, NW - 1)], 9)
+        send(mx.at[b, s], mx.at[b, s], 43 + s, {"branch": 1 - b})
+
+    arrived(rg.at[:, 0], 37)
+    send(rg.at[:, w_far], rg.at[:, w_far], 38, other_core)
+
+    for s in range(2):
+        arrived(mx.at[0, s], 43 + s)
+        x = mm(mx[0, s], mw_ref[0:128]) + mm(mx[1, s], mw_ref[128:256])
+        x = mn[:, s, :, cols].astype(F32).reshape(256, 128) + x
+        ao[:, s] = x.reshape(32, 8, 128).astype(BF)
+        mo[s, r] = ao[r, s]
+        row_peers(lambda peer: send(ao.at[peer, s], mo.at[s, r], 45 + s, {"row": peer}))
+
+    arrived(rg.at[:, 0], 36)
+    arrived(rg.at[:, 0], 38)
     for s in range(2):
         x = rg[:, :, s].astype(F32).reshape(32, 32, 128)
         x = jnp.transpose(x, (1, 0, 2)).astype(BF)
@@ -336,20 +391,12 @@
 
     lax.fori_loop(0, 16, outer_step, 0)
 
-    arrived(bk.at[pl.ds(0, NR - 1)], 6)
+    arrived(bk.at[pl.ds(0, NR - 1)], 39)
     xs[...] = jnp.transpose(bk[...].astype(F32), (1, 0, 2)).astype(BF)
     xr[q] = xs[pl.ds(2 * q, 2)]
     for k in range(1, NQ):
         peer = lax.rem(q + k, NQ)
-        send(xs.at[pl.ds(2 * peer, 2)], xr.at[q], 10, {"seq": peer})
-
-    for s in range(2):
-        arrived(mx.at[0, s], 13 + s)
-        x = mm(mx[0, s], mw_ref[0:128]) + mm(mx[1, s], mw_ref[128:256])
-        x = mn[:, s, :, cols].astype(F32).reshape(256, 128) + x
-        ao[:, s] = x.reshape(32, 8, 128).astype(BF)
-        mo[s, r] = ao[r, s]
-        row_peers(lambda peer: send(ao.at[peer, s], mo.at[s, r], 15 + s, {"row": peer}))
+        send(xs.at[pl.ds(2 * peer, 2)], xr.at[q], 40, {"seq": peer})
 
     for n in range(4):
         x = (mm(oot[...], pq[n]) * (1.0 / 256.0)).astype(BF)
@@ -358,9 +405,10 @@
     orb[q] = ob[q]
     for k in range(1, NQ):
         peer = lax.rem(q + k, NQ)
-        send(ob.at[peer], orb.at[q], 12, {"seq": peer})
-
-    arrived(w.at[pl.ds(0, NQ - 1)], 2)
+        send(ob.at[peer], orb.at[q], 42, {"seq": peer})
+
+    for k, c in ((7, 1), (8, 0), (10, 0), (11, 1)):
+        arrived(w_part(q, c), k)
     out_w = w[:, 32:64].astype(F32).reshape(128, 128)
     out_w = jnp.transpose(out_w).astype(BF)
     trans_gain = column(cn_ref[...])
@@ -369,7 +417,7 @@
     )
     tri_row = jnp.concatenate([tin[2 * q + i, :, cols] for i in range(2)], axis=1)
     gate = jax.nn.sigmoid(mm(w[:, 0:32].reshape(128, 128), tri_row))
-    arrived(xr.at[pl.ds(0, NQ - 1)], 10)
+    arrived(xr.at[pl.ds(0, NQ - 1)], 40)
     row_tri = jnp.concatenate(
         [xr[:, i].astype(F32).reshape(128, 128) for i in range(2)], axis=1
     )
@@ -386,47 +434,58 @@
     fb[pl.ds(2 * q, 2)] = pn[q]
     for k in range(1, NQ):
         peer = lax.rem(q + k, NQ)
-        send(pn.at[peer], fb.at[pl.ds(2 * q, 2)], 11, {"seq": peer})
-
-    arrived(orb.at[pl.ds(0, NQ - 1)], 12)
+        send(pn.at[peer], fb.at[pl.ds(2 * q, 2)], 41, {"seq": peer})
+
+    arrived(orb.at[pl.ds(0, NQ - 1)], 42)
     update = orb[0].astype(F32)
     for k in range(1, NQ):
         update = update + orb[k].astype(F32)
     update = update.astype(BF).astype(F32)
-    arrived(fb.at[pl.ds(0, 6)], 11)
+    arrived(fb.at[pl.ds(0, 6)], 41)
     update = update + fb[...].astype(F32)
     pair_ref[...] = jnp.transpose(update, (1, 0, 2)).reshape(256, 128).astype(BF)
 
     for s in range(2):
-        arrived(mo.at[s, pl.ds(0, NR - 1)], 15 + s)
+        arrived(mo.at[s, pl.ds(0, NR - 1)], 45 + s)
         msa_ref[256 * s : 256 * s + 256] = mo[s].astype(F32).reshape(256, 128).astype(BF)
 
+    for c in range(2):
+        for k in (0, 2, 4):
+            left_here(g_part(q, c), k + c)
+            left_here(w_part(q, c), 6 + k + c)
+    for n in range(8):
+        left_here(bf.at[0, pl.ds(0, NW if n else NW - 1)], 13 + n)
+    for n in range(4):
+        left_here(bf.at[0, pl.ds(0, NW)], 21 + n)
+        left_here(bf.at[0, pl.ds(0, NW)], 26 + n)
+    for k in (25, 30, 31, 32):
+        left_here(bf.at[0, pl.ds(0, 4 * NW)], k)
     for k, view in (
-        (0, g.at[pl.ds(0, NQ - 1)]),
-        (1, mn.at[pl.ds(0, NR - 1)]),
-        (2, w.at[pl.ds(0, NQ - 1)]),
-        (3, lb.at[pl.ds(0, NR - 1)]),
-        (6, bk.at[pl.ds(0, NR - 1)]),
-        (8, rg.at[pl.ds(0, NZ - 1), 0]),
-        (9, rg.at[:, pl.ds(0, NW - 1)]),
-        (10, xr.at[pl.ds(0, NQ - 1)]),
-        (11, fb.at[pl.ds(0, 6)]),
-        (12, orb.at[pl.ds(0, NQ - 1)]),
-        (13, mx.at[0, 0]),
-        (14, mx.at[0, 0]),
-        (15, mo.at[0, pl.ds(0, NR - 1)]),
-        (16, mo.at[0, pl.ds(0, NR - 1)]),
-        (17, bf.at[0, pl.ds(0, NW - 1)]),
+        (12, mn.at[pl.ds(0, NR - 1)]),
+        (33, lb.at[pl.ds(0, NR - 1)]),
+        (35, rg.at[pl.ds(0, NZ - 1), 0]),
+        (36, rg.at[:, 0]),
+        (37, rg.at[:, 0]),
+        (38, rg.at[:, 0]),
+        (39, bk.at[pl.ds(0, NR - 1)]),
+        (40, xr.at[pl.ds(0, NQ - 1)]),
+        (41, fb.at[pl.ds(0, 6)]),
+        (42, orb.at[pl.ds(0, NQ - 1)]),
+        (43, mx.at[0, 0]),
+        (44, mx.at[0, 0]),
+        (45, mo.at[0, pl.ds(0, NR - 1)]),
+        (46, mo.at[0, pl.ds(0, NR - 1)]),
     ):
         left_here(view, k)
-    for dz in range(1, NZ):
-        left_here(bf.at[0, pl.ds(0, NW)], 17 + dz)
-    for k in range(1, NQ):
-        left_here(bf.at[0], 24 + k)
 
     @pl.when(inside)
     def _():
-        left_here(lb.at[pl.ds(0, NR - 1)], 4)
+        left_here(lb.at[pl.ds(0, NR - 1)], 34)
+
+
+def hand_over(msa_in, pair_in, msa_out, pair_out):
+    msa_out[...] = msa_in[...]
+    pair_out[...] = pair_in[...]
 
 
 def shards(
@@ -496,6 +555,7 @@
             vm((16, 8, 256), BF),
             vm((4, 32, 8, 256), BF),
             vm((32, 2, 8, 256), BF),
+            vm((2, 256, 256), BF),
             vm((64, 256), F32),
             vm((256, 64), BF),
             vm((2, 4, 256, 128), BF),
@@ -514,13 +574,22 @@
             vm((32, 2, 8, 128), BF),
             vm((2, 32, 8, 128), BF),
             pltpu.SemaphoreType.DMA((17,)),
-            pltpu.SemaphoreType.DMA((28,)),
-            pltpu.SemaphoreType.DMA((28,)),
+            pltpu.SemaphoreType.DMA((47,)),
+            pltpu.SemaphoreType.DMA((47,)),
         ],
         compiler_params=pltpu.CompilerParams(
             collective_id=0, has_side_effects=True, vmem_limit_bytes=67_043_328
         ),
     )(*operands)
+    msa, pair = pl.pallas_call(
+        hand_over,
+        out_shape=(
+            jax.ShapeDtypeStruct((512, 128), BF),
+            jax.ShapeDtypeStruct((256, 128), BF),
+        ),
+        in_specs=[pl.BlockSpec(memory_space=pltpu.VMEM)] * 2,
+        out_specs=[pl.BlockSpec(memory_space=pltpu.VMEM)] * 2,
+    )(msa, pair)
     return msa.reshape(64, 8, 128), pair.reshape(32, 8, 128)
 
 

time: 59.1 us -> 55.5 us (0.939)
  the two profiles are of different devices: /device:TPU:1 before, /device:TPU:8 now
where the time goes in v5:
time: 55.5 us; the launch traced here: 55.4 us
  Pallas kernels  54.7 us (99%)
  between operations  0.65 us (1%)
    pallas_call x1, Pallas kernels, shards(): pl.pallas_call(body, out_shape=(jax.ShapeDtypeStruct((512, 128), BF), jax...  53.1 us
    pallas_call x1, Pallas kernels, shards(): pl.pallas_call(hand_over, out_shape=(jax.ShapeDtypeStruct((512, 128), BF)...  1.59 us

profile of v5, /device:TPU:8, one launch (start us, length us, event | category | flops | bytes accessed | tf_op | source)
XLA Modules:
  0.0 55.4 jit_solution(17281179258754944532)
XLA Ops:
  0.6 53.1 %shard_map.176 = (bf16[512,128]{1,0:T(8,128)(2,1)}, bf16[256,128]{1,0:T(8,128)(2,1)}) custom-call(bf16[2,32,8,256]{3,2,1,0:T(8,128)(2,1)} %bitcast.11, bf16[32,8,256]{2,1,0:T(8,128)(2,1)} %p_hbm.1, f32[1,256]{1,0:T(1,128)} %bitcast.15, f32[1,256]{1,0:T(1,128)} %bitcast.16, bf16[256,4,256]{2,1,0:T(4,128)(2,1)} %aw_hbm.1, bf16[256,256]{1,0:T(8,128)(2,1)} %mw_hbm.1, ...), custom_call_target="tpu_custom_call" | custom-call | tf_op jit(solution)/shard_map/pallas_call | solution.py:533
  53.8 1.6 %shard_map.177 = (bf16[512,128]{1,0:T(8,128)(2,1)}, bf16[256,128]{1,0:T(8,128)(2,1)}) custom-call(bf16[512,128]{1,0:T(8,128)(2,1)} %get-tuple-element.6.msa_in, bf16[256,128]{1,0:T(8,128)(2,1)} %get-tuple-element.7.pair_in), custom_call_target="tpu_custom_call" | custom-call | tf_op jit(solution)/shard_map/pallas_call | solution.py:584

commit v6 on v5

--- a/solution.py
+++ b/solution.py
@@ -253,10 +253,10 @@
 
     arrived(g_part(q, 0), 2)
     arrived(g_part(q, 0), 4)
-    acc = lax.fori_loop(0, 4, bias_row, jnp.zeros((8, 256), F32))
+    acc = lax.fori_loop(0, 4, bias_row, jnp.zeros((8, 256), F32), unroll=4)
     arrived(g_part(q, 1), 1)
     arrived(g_part(q, 1), 5)
-    bs[...] = lax.fori_loop(4, 8, bias_row, acc).astype(BF)
+    bs[...] = lax.fori_loop(4, 8, bias_row, acc, unroll=4).astype(BF)
     bf[q, r] = bs[...]
     for dz in range(NZ):
         for dw in range(NW):
@@ -271,7 +271,7 @@
         rt[i] = lin[64:96] * jax.nn.sigmoid(lin[96:128])
         return carry
 
-    lax.fori_loop(0, 8, tri_row_step, 0)
+    lax.fori_loop(0, 8, tri_row_step, 0, unroll=4)
     ls[...] = jnp.transpose(lt[...], (1, 0, 2)).astype(BF)
     rs[...] = jnp.transpose(rt[...], (1, 0, 2)).astype(BF)
     lb[r] = ls[r]
@@ -289,11 +289,9 @@
         rg[zi, wi, s] = jnp.where(b == 0, right[:, :128], right[:, 128:]).astype(BF)
         nm[s] = (x * ag_ref[...]).astype(BF)
 
-    def z_peers(k, carry):
-        send(rg.at[zi, wi], rg.at[zi, wi], 35, {"row": lax.rem(zi + k, NZ) * NW + wi})
-        return carry
-
-    lax.fori_loop(1, NZ, z_peers, 0)
+    for k in (1, 7, 2, 6, 3, 5, 4):
+        peer = {"row": lax.rem(zi + k, NZ) * NW + wi}
+        send(rg.at[zi, wi], rg.at[zi, wi], 46 + k, peer)
     pass_on(w_part, 6)
     for s in range(2):
         qkv[s, 0] = (mm(nm[s], awt[0]) * (32.0**-0.5)).astype(BF)
@@ -309,18 +307,36 @@
         part = group(q, dz)
         send(part, part, 21 + dz if dz < 4 else 25, right_nb)
         send(part, part, 33 - dz if dz >= 4 else 30, left_nb)
-    for n in range(4):
+    def relay(n):
         arrived(bf.at[0, pl.ds(0, NW)], 21 + n)
         send(group(q_left, n), group(q_left, n), 31, right_nb)
         arrived(bf.at[0, pl.ds(0, NW)], 26 + n)
         send(group(q_right, 7 - n), group(q_right, 7 - n), 32, left_nb)
 
-    arrived(rg.at[pl.ds(0, NZ - 1), 0], 35)
+    relay(0)
+    relay(1)
+
     w_core = wi + 1 - 2 * (wi % 2)
     w_far = lax.rem(wi + 2, NW)
     other_core = {"row": zi * NW + w_core}
-    send(rg.at[:, wi], rg.at[:, wi], 37, {"row": zi * NW + w_far})
-    send(rg.at[:, wi], rg.at[:, wi], 36, other_core)
+    near, rest = (0, 1, 7, 2, 6), (3, 5, 4)
+
+    def onward(distances, slot, k, where):
+        for dz in distances:
+            block = rg.at[lax.rem(zi + NZ - dz, NZ), slot]
+            send(block, block, k, where)
+
+    def from_z(distances, k):
+        for dz in distances:
+            if dz:
+                arrived(rg.at[0, 0], 46 + dz)
+            onward((dz,), wi, k, {"row": zi * NW + w_far})
+            onward((dz,), wi, 36, other_core)
+
+    from_z(near, 37)
+    relay(2)
+    relay(3)
+    from_z(rest, 35)
 
     arrived(lb.at[pl.ds(0, NR - 1)], 33)
 
@@ -359,8 +375,18 @@
         mx[b, s] = (qkv[s, 3].astype(F32) * value).astype(BF)
         send(mx.at[b, s], mx.at[b, s], 43 + s, {"branch": 1 - b})
 
-    arrived(rg.at[:, 0], 37)
-    send(rg.at[:, w_far], rg.at[:, w_far], 38, other_core)
+    arrived(rg.at[pl.ds(0, 5), 0], 37)
+    onward(near, w_far, 38, other_core)
+    arrived(rg.at[pl.ds(0, 3), 0], 35)
+    onward(rest, w_far, 38, other_core)
+
+    arrived(rg.at[:, 0], 36)
+    arrived(rg.at[:, 0], 38)
+    for s in range(2):
+        x = rg[:, :, s].astype(F32).reshape(32, 32, 128)
+        x = jnp.transpose(x, (1, 0, 2)).astype(BF)
+        for d in range(32):
+            rgt[32 * s : 32 * s + 32, 128 * d : 128 * d + 128] = x[d]
 
     for s in range(2):
         arrived(mx.at[0, s], 43 + s)
@@ -370,13 +396,12 @@
         mo[s, r] = ao[r, s]
         row_peers(lambda peer: send(ao.at[peer, s], mo.at[s, r], 45 + s, {"row": peer}))
 
-    arrived(rg.at[:, 0], 36)
-    arrived(rg.at[:, 0], 38)
-    for s in range(2):
-        x = rg[:, :, s].astype(F32).reshape(32, 32, 128)
-        x = jnp.transpose(x, (1, 0, 2)).astype(BF)
-        for d in range(32):
-            rgt[32 * s : 32 * s + 32, 128 * d : 128 * d + 128] = x[d]
+    arrived(bk.at[pl.ds(0, NR - 1)], 39)
+    xs[...] = jnp.transpose(bk[...].astype(F32), (1, 0, 2)).astype(BF)
+    xr[q] = xs[pl.ds(2 * q, 2)]
+    for k in range(1, NQ):
+        peer = lax.rem(q + k, NQ)
+        send(xs.at[pl.ds(2 * peer, 2)], xr.at[q], 40, {"seq": peer})
 
     def outer_step(n, carry):
         x = mm(lxt[...], rgt[:, pl.ds(pl.multiple_of(n * 256, 256), 256)]).astype(BF)
@@ -389,14 +414,7 @@
                 ] = x[32 * i : 32 * i + 32, 128 * d : 128 * d + 128]
         return carry
 
-    lax.fori_loop(0, 16, outer_step, 0)
-
-    arrived(bk.at[pl.ds(0, NR - 1)], 39)
-    xs[...] = jnp.transpose(bk[...].astype(F32), (1, 0, 2)).astype(BF)
-    xr[q] = xs[pl.ds(2 * q, 2)]
-    for k in range(1, NQ):
-        peer = lax.rem(q + k, NQ)
-        send(xs.at[pl.ds(2 * peer, 2)], xr.at[q], 40, {"seq": peer})
+    lax.fori_loop(0, 16, outer_step, 0, unroll=8)
 
     for n in range(4):
         x = (mm(oot[...], pq[n]) * (1.0 / 256.0)).astype(BF)
@@ -455,6 +473,8 @@
             left_here(w_part(q, c), 6 + k + c)
     for n in range(8):
         left_here(bf.at[0, pl.ds(0, NW if n else NW - 1)], 13 + n)
+    for n in range(1, NZ):
+        left_here(rg.at[0, 0], 46 + n)
     for n in range(4):
         left_here(bf.at[0, pl.ds(0, NW)], 21 + n)
         left_here(bf.at[0, pl.ds(0, NW)], 26 + n)
@@ -463,9 +483,9 @@
     for k, view in (
         (12, mn.at[pl.ds(0, NR - 1)]),
         (33, lb.at[pl.ds(0, NR - 1)]),
-        (35, rg.at[pl.ds(0, NZ - 1), 0]),
+        (35, rg.at[pl.ds(0, 3), 0]),
         (36, rg.at[:, 0]),
-        (37, rg.at[:, 0]),
+        (37, rg.at[pl.ds(0, 5), 0]),
         (38, rg.at[:, 0]),
         (39, bk.at[pl.ds(0, NR - 1)]),
         (40, xr.at[pl.ds(0, NQ - 1)]),
@@ -574,8 +594,8 @@
             vm((32, 2, 8, 128), BF),
             vm((2, 32, 8, 128), BF),
             pltpu.SemaphoreType.DMA((17,)),
-            pltpu.SemaphoreType.DMA((47,)),
-            pltpu.SemaphoreType.DMA((47,)),
+            pltpu.SemaphoreType.DMA((54,)),
+            pltpu.SemaphoreType.DMA((54,)),
         ],
         compiler_params=pltpu.CompilerParams(
             collective_id=0, has_side_effects=True, vmem_limit_bytes=67_043_328

time: 55.5 us -> 52 us (0.937)
  the two profiles are of different devices: /device:TPU:8 before, /device:TPU:1 now
where the time goes in v6:
time: 52 us; the launch traced here: 51.5 us
  Pallas kernels  50.8 us (98%)
  between operations  0.65 us (1%)
    pallas_call x1, Pallas kernels, shards(): pl.pallas_call(body, out_shape=(jax.ShapeDtypeStruct((512, 128), BF), jax...  49.2 us
    pallas_call x1, Pallas kernels, shards(): pl.pallas_call(hand_over, out_shape=(jax.ShapeDtypeStruct((512, 128), BF)...  1.59 us

profile of v6, /device:TPU:1, one launch (start us, length us, event | category | flops | bytes accessed | tf_op | source)
XLA Modules:
  0.0 51.5 jit_solution(6851706401943155199)
XLA Ops:
  0.6 49.2 %shard_map.176 = (bf16[512,128]{1,0:T(8,128)(2,1)}, bf16[256,128]{1,0:T(8,128)(2,1)}) custom-call(bf16[2,32,8,256]{3,2,1,0:T(8,128)(2,1)} %bitcast.11, bf16[32,8,256]{2,1,0:T(8,128)(2,1)} %p_hbm.1, f32[1,256]{1,0:T(1,128)} %bitcast.15, f32[1,256]{1,0:T(1,128)} %bitcast.16, bf16[256,4,256]{2,1,0:T(4,128)(2,1)} %aw_hbm.1, bf16[256,256]{1,0:T(8,128)(2,1)} %mw_hbm.1, ...), custom_call_target="tpu_custom_call" | custom-call | tf_op jit(solution)/shard_map/pallas_call | solution.py:553
  49.9 1.6 %shard_map.177 = (bf16[512,128]{1,0:T(8,128)(2,1)}, bf16[256,128]{1,0:T(8,128)(2,1)}) custom-call(bf16[512,128]{1,0:T(8,128)(2,1)} %get-tuple-element.6.msa_in, bf16[256,128]{1,0:T(8,128)(2,1)} %get-tuple-element.7.pair_in), custom_call_target="tpu_custom_call" | custom-call | tf_op jit(solution)/shard_map/pallas_call | solution.py:604

commit v7 on v6

--- a/solution.py
+++ b/solution.py
@@ -187,11 +187,10 @@
         return w.at[slot, pl.ds(160 * c, 160)]
 
     def row_peers(do):
-        def step(k, carry):
-            do(lax.rem(r + k, NR))
-            return carry
-
-        lax.fori_loop(1, NR, step, 0)
+        for dz in (4, 3, 5, 2, 6, 1, 7, 0):
+            for dw in (2, 3, 1, 0):
+                if dz or dw:
+                    do(lax.rem(zi + dz, NZ) * NW + lax.rem(wi + dw, NW))
 
     barrier = pltpu.get_barrier_semaphore()
     row_peers(lambda peer: signal({"row": peer}))
@@ -258,13 +257,11 @@
     arrived(g_part(q, 1), 5)
     bs[...] = lax.fori_loop(4, 8, bias_row, acc, unroll=4).astype(BF)
     bf[q, r] = bs[...]
-    for dz in range(NZ):
-        for dw in range(NW):
+    for dz in (4, 3, 5, 2, 6, 1, 7, 0):
+        for dw in (2, 3, 1, 0):
             if dz or dw:
                 peer = lax.rem(zi + dz, NZ) * NW + lax.rem(wi + dw, NW)
                 send(bs, bf.at[q, r], 13 + dz, {"row": peer})
-    both_ways(w_part, 6)
-
     def tri_row_step(i, carry):
         lin = mm(ti_ref[...].reshape(128, 128), tin[i])
         lt[i] = lin[0:32] * jax.nn.sigmoid(lin[32:64])
@@ -281,6 +278,8 @@
     def _():
         rb[r % (NR // 2)] = rs[r]
         row_peers(lambda peer: send(rs.at[peer], rb.at[r % (NR // 2)], 34, {"row": peer}))
+
+    both_ways(w_part, 6)
 
     arrived(mn.at[pl.ds(0, NR - 1)], 12)
     for s in range(2):
@@ -399,7 +398,7 @@
     arrived(bk.at[pl.ds(0, NR - 1)], 39)
     xs[...] = jnp.transpose(bk[...].astype(F32), (1, 0, 2)).astype(BF)
     xr[q] = xs[pl.ds(2 * q, 2)]
-    for k in range(1, NQ):
+    for k in (2, 1, 3):
         peer = lax.rem(q + k, NQ)
         send(xs.at[pl.ds(2 * peer, 2)], xr.at[q], 40, {"seq": peer})
 
@@ -421,7 +420,7 @@
         for i in range(2):
             ob[:, 2 * n + i] = x[:, 128 * i : 128 * i + 128].reshape(4, 32, 128)
     orb[q] = ob[q]
-    for k in range(1, NQ):
+    for k in (2, 1, 3):
         peer = lax.rem(q + k, NQ)
         send(ob.at[peer], orb.at[q], 42, {"seq": peer})
 
@@ -450,7 +449,7 @@
     for i in range(2):
         pn[:, i] = moved[:, 128 * i : 128 * i + 128].reshape(4, 32, 128)
     fb[pl.ds(2 * q, 2)] = pn[q]
-    for k in range(1, NQ):
+    for k in (2, 1, 3):
         peer = lax.rem(q + k, NQ)
         send(pn.at[peer], fb.at[pl.ds(2 * q, 2)], 41, {"seq": peer})
 
@@ -503,9 +502,15 @@
         left_here(lb.at[pl.ds(0, NR - 1)], 34)
 
 
-def hand_over(msa_in, pair_in, msa_out, pair_out):
-    msa_out[...] = msa_in[...]
-    pair_out[...] = pair_in[...]
+def hand_over(msa_in, pair_in, msa_out, pair_out, sems):
+    copies = (
+        pltpu.make_async_copy(msa_in, msa_out, sems.at[0]),
+        pltpu.make_async_copy(pair_in, pair_out, sems.at[1]),
+    )
+    for copy in copies:
+        copy.start()
+    for copy in copies:
+        copy.wait()
 
 
 def shards(
@@ -552,10 +557,7 @@
     held[5] = vm((256, 128), BF)
     msa, pair = pl.pallas_call(
         body,
-        out_shape=(
-            jax.ShapeDtypeStruct((512, 128), BF),
-            jax.ShapeDtypeStruct((256, 128), BF),
-        ),
+        out_shape=(pltpu.VMEM((512, 128), BF), pltpu.VMEM((256, 128), BF)),
         in_specs=[pl.BlockSpec(memory_space=pltpu.HBM)] * len(operands),
         out_specs=[pl.BlockSpec(memory_space=pltpu.VMEM)] * 2,
         scratch_shapes=held
@@ -598,9 +600,9 @@
             pltpu.SemaphoreType.DMA((54,)),
         ],
         compiler_params=pltpu.CompilerParams(
-            collective_id=0, has_side_effects=True, vmem_limit_bytes=67_043_328
+            collective_id=0, has_side_effects=True, vmem_limit_bytes=48 * 2**20
         ),
-    )(*operands)
+    )(*(pltpu.with_memory_space_constraint(x, pltpu.HBM) for x in operands))
     msa, pair = pl.pallas_call(
         hand_over,
         out_shape=(
@@ -608,8 +610,9 @@
             jax.ShapeDtypeStruct((256, 128), BF),
         ),
         in_specs=[pl.BlockSpec(memory_space=pltpu.VMEM)] * 2,
-        out_specs=[pl.BlockSpec(memory_space=pltpu.VMEM)] * 2,
-    )(msa, pair)
+        out_specs=[pl.BlockSpec(memory_space=pltpu.HBM)] * 2,
+        scratch_shapes=[pltpu.SemaphoreType.DMA((2,))],
+    )(*(pltpu.with_memory_space_constraint(x, pltpu.VMEM) for x in (msa, pair)))
     return msa.reshape(64, 8, 128), pair.reshape(32, 8, 128)
 
 

time: 52 us -> 49.3 us (0.948)
  Pallas kernels: 50.8 us -> 48.1 us
    pallas_call x1, Pallas kernels: 49.2 us -> 47.4 us  [shards(): pl.pallas_call(body, out_shape=(pltpu.VMEM((512, 128), BF), pltpu.VMEM((2...]
    pallas_call x1, Pallas kernels: 1.59 us -> 0.69 us  [shards(): pl.pallas_call(hand_over, out_shape=(jax.ShapeDtypeStruct((512, 128), BF)...]
where the time goes in v7:
time: 49.3 us; the launch traced here: 48.8 us
  Pallas kernels  48.1 us (98%)
  between operations  0.65 us (1%)
    pallas_call x1, Pallas kernels, shards(): pl.pallas_call(body, out_shape=(pltpu.VMEM((512, 128), BF), pltpu.VMEM((2...  47.4 us

profile of v7, /device:TPU:1, one launch (start us, length us, event | category | flops | bytes accessed | tf_op | source)
XLA Modules:
  0.0 48.8 jit_solution(18248338744950477365)
XLA Ops:
  0.6 47.4 %shard_map.176 = (bf16[512,128]{1,0:T(8,128)(2,1)S(1)}, bf16[256,128]{1,0:T(8,128)(2,1)S(1)}) custom-call(bf16[2,32,8,256]{3,2,1,0:T(8,128)(2,1)} %bitcast.11, bf16[32,8,256]{2,1,0:T(8,128)(2,1)} %p_hbm.1, f32[1,256]{1,0:T(1,128)} %bitcast.15, f32[1,256]{1,0:T(1,128)} %bitcast.16, bf16[256,4,256]{2,1,0:T(4,128)(2,1)} %aw_hbm.1, bf16[256,256]{1,0:T(8,128)(2,1)} %mw_hbm.1, ...), custom_call_target="tpu_custom_call" | custom-call | tf_op jit(solution)/shard_map/pallas_call | solution.py:558
  48.1 0.7 %shard_map.177 = (bf16[512,128]{1,0:T(8,128)(2,1)}, bf16[256,128]{1,0:T(8,128)(2,1)}) custom-call(bf16[512,128]{1,0:T(8,128)(2,1)S(1)} %get-tuple-element.6.msa_in, bf16[256,128]{1,0:T(8,128)(2,1)S(1)} %get-tuple-element.7.pair_in), custom_call_target="tpu_custom_call" | custom-call | tf_op jit(solution)/shard_map/pallas_call | solution.py:606

commit v8 on v7

--- a/solution.py
+++ b/solution.py
@@ -118,6 +118,55 @@
     inside = (r // (NR // 2)) == b
     cols = pl.ds(pl.multiple_of(b * 128, 128), 128)
 
+    def signal(where):
+        pl.semaphore_signal(
+            barrier, inc=1, device_id=where, device_id_type=pl.DeviceIdType.MESH
+        )
+
+    def send(src, dst, k, where):
+        pltpu.make_async_remote_copy(
+            src_ref=src,
+            dst_ref=dst,
+            send_sem=ss.at[k],
+            recv_sem=rv.at[k],
+            device_id=where,
+            device_id_type=pl.DeviceIdType.MESH,
+        ).start()
+
+    def arrived(view, k):
+        pltpu.make_async_copy(view, view, rv.at[k]).wait()
+
+    def left_here(view, k):
+        pltpu.make_async_copy(view, view, ss.at[k]).wait()
+
+    right_nb = {"seq": lax.rem(q + 1, NQ)}
+    left_nb = {"seq": lax.rem(q + NQ - 1, NQ)}
+    q_right = lax.rem(q + 1, NQ)
+    q_left = lax.rem(q + NQ - 1, NQ)
+
+    def both_ways(view, k):
+        for c in range(2):
+            send(view(q, c), view(q, c), k + c, right_nb)
+            send(view(q, c), view(q, c), k + 2 + c, left_nb)
+
+    def pass_on(view, k):
+        arrived(view(q, 0), k)
+        send(view(q_left, 0), view(q_left, 0), k + 4, right_nb)
+        arrived(view(q, 1), k + 3)
+        send(view(q_right, 1), view(q_right, 1), k + 5, left_nb)
+
+    def g_part(slot, c):
+        return g.at[slot, pl.ds(4 * c, 4)]
+
+    def w_part(slot, c):
+        return w.at[slot, pl.ds(160 * c, 160)]
+
+    def row_peers(do):
+        for dz in (4, 3, 5, 2, 6, 1, 7, 0):
+            for dw in (2, 3, 1, 0):
+                if dz or dw:
+                    do(lax.rem(zi + dz, NZ) * NW + lax.rem(wi + dw, NW))
+
     loads = {}
     for n, (src, dst) in enumerate(
         (
@@ -141,62 +190,14 @@
         )
     ):
         loads[n] = pltpu.make_async_copy(src, dst, cs.at[n])
-        loads[n].start()
-
-    def signal(where):
-        pl.semaphore_signal(
-            barrier, inc=1, device_id=where, device_id_type=pl.DeviceIdType.MESH
-        )
-
-    def send(src, dst, k, where):
-        pltpu.make_async_remote_copy(
-            src_ref=src,
-            dst_ref=dst,
-            send_sem=ss.at[k],
-            recv_sem=rv.at[k],
-            device_id=where,
-            device_id_type=pl.DeviceIdType.MESH,
-        ).start()
-
-    def arrived(view, k):
-        pltpu.make_async_copy(view, view, rv.at[k]).wait()
-
-    def left_here(view, k):
-        pltpu.make_async_copy(view, view, ss.at[k]).wait()
-
-    right_nb = {"seq": lax.rem(q + 1, NQ)}
-    left_nb = {"seq": lax.rem(q + NQ - 1, NQ)}
-    q_right = lax.rem(q + 1, NQ)
-    q_left = lax.rem(q + NQ - 1, NQ)
-
-    def both_ways(view, k):
-        for c in range(2):
-            send(view(q, c), view(q, c), k + c, right_nb)
-            send(view(q, c), view(q, c), k + 2 + c, left_nb)
-
-    def pass_on(view, k):
-        arrived(view(q, 0), k)
-        send(view(q_left, 0), view(q_left, 0), k + 4, right_nb)
-        arrived(view(q, 1), k + 3)
-        send(view(q_right, 1), view(q_right, 1), k + 5, left_nb)
-
-    def g_part(slot, c):
-        return g.at[slot, pl.ds(4 * c, 4)]
-
-    def w_part(slot, c):
-        return w.at[slot, pl.ds(160 * c, 160)]
-
-    def row_peers(do):
-        for dz in (4, 3, 5, 2, 6, 1, 7, 0):
-            for dw in (2, 3, 1, 0):
-                if dz or dw:
-                    do(lax.rem(zi + dz, NZ) * NW + lax.rem(wi + dw, NW))
-
+    loads[0].start()
     barrier = pltpu.get_barrier_semaphore()
     row_peers(lambda peer: signal({"row": peer}))
     for k in range(1, NQ):
         signal({"seq": lax.rem(q + k, NQ)})
     signal({"branch": 1 - b})
+    for n in range(1, len(loads)):
+        loads[n].start()
 
     loads[0].wait()
     g[q] = jnp.transpose(p_ref[...].astype(F32), (1, 0, 2)).astype(BF)
@@ -304,17 +305,9 @@
     for dz in (0, 1, 7, 2, 6, 3, 5, 4):
         arrived(bf.at[0, pl.ds(0, NW if dz else NW - 1)], 13 + dz)
         part = group(q, dz)
+        send(part, part, 31 if dz < 4 else 32, {"seq": lax.rem(q + 2, NQ)})
         send(part, part, 21 + dz if dz < 4 else 25, right_nb)
         send(part, part, 33 - dz if dz >= 4 else 30, left_nb)
-    def relay(n):
-        arrived(bf.at[0, pl.ds(0, NW)], 21 + n)
-        send(group(q_left, n), group(q_left, n), 31, right_nb)
-        arrived(bf.at[0, pl.ds(0, NW)], 26 + n)
-        send(group(q_right, 7 - n), group(q_right, 7 - n), 32, left_nb)
-
-    relay(0)
-    relay(1)
-
     w_core = wi + 1 - 2 * (wi % 2)
     w_far = lax.rem(wi + 2, NW)
     other_core = {"row": zi * NW + w_core}
@@ -333,8 +326,6 @@
             onward((dz,), wi, 36, other_core)
 
     from_z(near, 37)
-    relay(2)
-    relay(3)
     from_z(rest, 35)
 
     arrived(lb.at[pl.ds(0, NR - 1)], 33)
@@ -360,8 +351,12 @@
             h = lax.rem(q + (0, 1, 3, 2)[k], NQ)
             if s == 0 and k == 1:
                 arrived(bf.at[0, pl.ds(0, 4 * NW)], 30)
+                for n in range(4):
+                    arrived(bf.at[0, pl.ds(0, NW)], 26 + n)
             if s == 0 and k == 2:
                 arrived(bf.at[0, pl.ds(0, 4 * NW)], 25)
+                for n in range(4):
+                    arrived(bf.at[0, pl.ds(0, NW)], 21 + n)
             if s == 0 and k == 3:
                 arrived(bf.at[0, pl.ds(0, 4 * NW)], 31)
                 arrived(bf.at[0, pl.ds(0, 4 * NW)], 32)
@@ -453,19 +448,6 @@
         peer = lax.rem(q + k, NQ)
         send(pn.at[peer], fb.at[pl.ds(2 * q, 2)], 41, {"seq": peer})
 
-    arrived(orb.at[pl.ds(0, NQ - 1)], 42)
-    update = orb[0].astype(F32)
-    for k in range(1, NQ):
-        update = update + orb[k].astype(F32)
-    update = update.astype(BF).astype(F32)
-    arrived(fb.at[pl.ds(0, 6)], 41)
-    update = update + fb[...].astype(F32)
-    pair_ref[...] = jnp.transpose(update, (1, 0, 2)).reshape(256, 128).astype(BF)
-
-    for s in range(2):
-        arrived(mo.at[s, pl.ds(0, NR - 1)], 45 + s)
-        msa_ref[256 * s : 256 * s + 256] = mo[s].astype(F32).reshape(256, 128).astype(BF)
-
     for c in range(2):
         for k in (0, 2, 4):
             left_here(g_part(q, c), k + c)
@@ -488,18 +470,32 @@
         (38, rg.at[:, 0]),
         (39, bk.at[pl.ds(0, NR - 1)]),
         (40, xr.at[pl.ds(0, NQ - 1)]),
-        (41, fb.at[pl.ds(0, 6)]),
-        (42, orb.at[pl.ds(0, NQ - 1)]),
         (43, mx.at[0, 0]),
         (44, mx.at[0, 0]),
-        (45, mo.at[0, pl.ds(0, NR - 1)]),
-        (46, mo.at[0, pl.ds(0, NR - 1)]),
     ):
         left_here(view, k)
 
     @pl.when(inside)
     def _():
         left_here(lb.at[pl.ds(0, NR - 1)], 34)
+
+    arrived(orb.at[pl.ds(0, NQ - 1)], 42)
+    update = orb[0].astype(F32)
+    for k in range(1, NQ):
+        update = update + orb[k].astype(F32)
+    update = update.astype(BF).astype(F32)
+    arrived(fb.at[pl.ds(0, 6)], 41)
+    update = update + fb[...].astype(F32)
+    pair_ref[...] = jnp.transpose(update, (1, 0, 2)).reshape(256, 128).astype(BF)
+
+    for s in range(2):
+        arrived(mo.at[s, pl.ds(0, NR - 1)], 45 + s)
+        msa_ref[256 * s : 256 * s + 256] = mo[s].astype(F32).reshape(256, 128).astype(BF)
+
+    left_here(fb.at[pl.ds(0, 6)], 41)
+    left_here(orb.at[pl.ds(0, NQ - 1)], 42)
+    for s in range(2):
+        left_here(mo.at[0, pl.ds(0, NR - 1)], 45 + s)
 
 
 def hand_over(msa_in, pair_in, msa_out, pair_out, sems):

time: 49.3 us -> 49 us (level)
  no operation moved by 1% of the time
where the time goes in v8:
time: 49 us; the launch traced here: 48.9 us
  Pallas kernels  48.3 us (99%)
  between operations  0.65 us (1%)
    pallas_call x1, Pallas kernels, shards(): pl.pallas_call(body, out_shape=(pltpu.VMEM((512, 128), BF), pltpu.VMEM((2...  47.6 us

profile of v8, /device:TPU:1, one launch (start us, length us, event | category | flops | bytes accessed | tf_op | source)
XLA Modules:
  0.0 48.9 jit_solution(7850932331032295814)
XLA Ops:
  0.6 47.6 %shard_map.176 = (bf16[512,128]{1,0:T(8,128)(2,1)S(1)}, bf16[256,128]{1,0:T(8,128)(2,1)S(1)}) custom-call(bf16[2,32,8,256]{3,2,1,0:T(8,128)(2,1)} %bitcast.11, bf16[32,8,256]{2,1,0:T(8,128)(2,1)} %p_hbm.1, f32[1,256]{1,0:T(1,128)} %bitcast.15, f32[1,256]{1,0:T(1,128)} %bitcast.16, bf16[256,4,256]{2,1,0:T(4,128)(2,1)} %aw_hbm.1, bf16[256,256]{1,0:T(8,128)(2,1)} %mw_hbm.1, ...), custom_call_target="tpu_custom_call" | custom-call | tf_op jit(solution)/shard_map/pallas_call | solution.py:554
  48.2 0.7 %shard_map.177 = (bf16[512,128]{1,0:T(8,128)(2,1)}, bf16[256,128]{1,0:T(8,128)(2,1)}) custom-call(bf16[512,128]{1,0:T(8,128)(2,1)S(1)} %get-tuple-element.6.msa_in, bf16[256,128]{1,0:T(8,128)(2,1)S(1)} %get-tuple-element.7.pair_in), custom_call_target="tpu_custom_call" | custom-call | tf_op jit(solution)/shard_map/pallas_call | solution.py:602

commit v9 on v8

--- a/solution.py
+++ b/solution.py
@@ -232,7 +232,7 @@
             )
     lxt[...] = jnp.transpose(lx[...]).astype(BF)
     loads[9].wait()
-    awf[...] = aw_ref[...].astype(F32).reshape(1024, 128)
+    awf[0:1024] = aw_ref[...].astype(F32).reshape(1024, 128)
     for t in range(4):
         awt[t] = awf[pl.ds(t, 256, stride=4)].astype(BF)
     loads[10].wait()
@@ -558,7 +558,7 @@
         out_specs=[pl.BlockSpec(memory_space=pltpu.VMEM)] * 2,
         scratch_shapes=held
         + [
-            vm((1024, 128), F32),
+            vm((1040, 128), F32),
             vm((4, 256, 128), BF),
             vm((128, 1024), BF),
             vm((4, 8, 32, 256), BF),

time: 49 us -> 49 us (level)
  no operation moved by 1% of the time
where the time goes in v9:
time: 49 us; the launch traced here: 48.9 us
  Pallas kernels  48.3 us (99%)
  between operations  0.65 us (1%)
    pallas_call x1, Pallas kernels, shards(): pl.pallas_call(body, out_shape=(pltpu.VMEM((512, 128), BF), pltpu.VMEM((2...  47.6 us

profile of v9, /device:TPU:1, one launch (start us, length us, event | category | flops | bytes accessed | tf_op | source)
XLA Modules:
  0.0 48.9 jit_solution(12779679026786676192)
XLA Ops:
  0.6 47.6 %shard_map.176 = (bf16[512,128]{1,0:T(8,128)(2,1)S(1)}, bf16[256,128]{1,0:T(8,128)(2,1)S(1)}) custom-call(bf16[2,32,8,256]{3,2,1,0:T(8,128)(2,1)} %bitcast.11, bf16[32,8,256]{2,1,0:T(8,128)(2,1)} %p_hbm.1, f32[1,256]{1,0:T(1,128)} %bitcast.15, f32[1,256]{1,0:T(1,128)} %bitcast.16, bf16[256,4,256]{2,1,0:T(4,128)(2,1)} %aw_hbm.1, bf16[256,256]{1,0:T(8,128)(2,1)} %mw_hbm.1, ...), custom_call_target="tpu_custom_call" | custom-call | tf_op jit(solution)/shard_map/pallas_call | solution.py:554
  48.2 0.7 %shard_map.177 = (bf16[512,128]{1,0:T(8,128)(2,1)}, bf16[256,128]{1,0:T(8,128)(2,1)}) custom-call(bf16[512,128]{1,0:T(8,128)(2,1)S(1)} %get-tuple-element.6.msa_in, bf16[256,128]{1,0:T(8,128)(2,1)S(1)} %get-tuple-element.7.pair_in), custom_call_target="tpu_custom_call" | custom-call | tf_op jit(solution)/shard_map/pallas_call | solution.py:602
